TPU v7x, 32 devices: a whole 2x2x4 slice. The times are simulated.
32 devices in a mesh: dp: 8 (over z, x), branch: 4 (over y, core).
Axes of the slice: x: 2, y: 2, z: 4, core: 2. Of those that a mesh axis runs over, the one named last changes fastest.
Arguments:
- inputs: bfloat16 [16, 512, 2048], P('dp', 'branch'), may hold values from -6 to 6
- segments: int32 [16, 512], P('dp'), may hold values from 0 to 4, as said below
- out_grad: bfloat16 [16, 512, 2048], P('dp', 'branch'), may hold values from -6 to 6
- layer_params: float32 [3, 2048], replicated, may hold values from -0.5 to 2.4
- attend_weight: float32 [3, 2048, 2048], P(None, 'dp', 'branch'), may hold values from -0.125 to 0.125
- attend_bias: float32 [3, 2048], P(None, ('branch', 'dp')), may hold values from -1.5 to 1.5
- output_weight: float32 [2048, 2048], P('branch', 'dp'), may hold values from -0.75 to 0.75
- expand_weight: float32 [2048, 8192], P('dp', 'branch'), may hold values from -0.125 to 0.125
- expand_bias: float32 [8192], P(('branch', 'dp')), may hold values from -1.5 to 1.5
- shrink_weight: float32 [8192, 2048], P('branch', 'dp'), may hold values from -0.0625 to 0.0625
- mean_layer: float32 [3, 2048], replicated, may hold values from -10 to 10
- mean_attend_weight: float32 [3, 2048, 2048], P(None, 'dp', 'branch'), may hold values from -6 to 6
- mean_attend_bias: float32 [3, 2048], P(None, ('branch', 'dp')), may hold values from -6 to 6
- mean_output_weight: float32 [2048, 2048], P('branch', 'dp'), may hold values from -6 to 6
- mean_expand_weight: float32 [2048, 8192], P('dp', 'branch'), may hold values from -6 to 6
- mean_expand_bias: float32 [8192], P(('branch', 'dp')), may hold values from -6 to 6
- mean_shrink_weight: float32 [8192, 2048], P('branch', 'dp'), may hold values from -6 to 6
- square_layer: float32 [3, 2048], replicated, may hold values from 4 to 16
- square_attend_weight: float32 [3, 2048, 2048], P(None, 'dp', 'branch'), may hold values from 1 to 4
- square_attend_bias: float32 [3, 2048], P(None, ('branch', 'dp')), may hold values from 1 to 4
- square_output_weight: float32 [2048, 2048], P('branch', 'dp'), may hold values from 1 to 4
- square_expand_weight: float32 [2048, 8192], P('dp', 'branch'), may hold values from 1 to 4
- square_expand_bias: float32 [8192], P(('branch', 'dp')), may hold values from 1 to 4
- square_shrink_weight: float32 [8192, 2048], P('branch', 'dp'), may hold values from 1 to 4
Outputs:
- block_output: bfloat16 [16, 512, 2048], P('dp', 'branch')
- grad_inputs: bfloat16 [16, 512, 2048], P('dp', 'branch')
- grad_norm: float32 [1], replicated
- next_layer: float32 [3, 2048], replicated
- next_attend_weight: float32 [3, 2048, 2048], P(None, 'dp', 'branch')
- next_attend_bias: float32 [3, 2048], P(None, ('branch', 'dp'))
- next_output_weight: float32 [2048, 2048], P('branch', 'dp')
- next_expand_weight: float32 [2048, 8192], P('dp', 'branch')
- next_expand_bias: float32 [8192], P(('branch', 'dp'))
- next_shrink_weight: float32 [8192, 2048], P('branch', 'dp')
- next_mean_layer: float32 [3, 2048], replicated
- next_mean_attend_weight: float32 [3, 2048, 2048], P(None, 'dp', 'branch')
- next_mean_attend_bias: float32 [3, 2048], P(None, ('branch', 'dp'))
- next_mean_output_weight: float32 [2048, 2048], P('branch', 'dp')
- next_mean_expand_weight: float32 [2048, 8192], P('dp', 'branch')
- next_mean_expand_bias: float32 [8192], P(('branch', 'dp'))
- next_mean_shrink_weight: float32 [8192, 2048], P('branch', 'dp')
- next_square_layer: float32 [3, 2048], replicated
- next_square_attend_weight: float32 [3, 2048, 2048], P(None, 'dp', 'branch')
- next_square_attend_bias: float32 [3, 2048], P(None, ('branch', 'dp'))
- next_square_output_weight: float32 [2048, 2048], P('branch', 'dp')
- next_square_expand_weight: float32 [2048, 8192], P('dp', 'branch')
- next_square_expand_bias: float32 [8192], P(('branch', 'dp'))
- next_square_shrink_weight: float32 [8192, 2048], P('branch', 'dp')
- copy_attend_weight: bfloat16 [3, 2048, 2048], P(None, 'dp', 'branch')
- copy_output_weight: bfloat16 [2048, 2048], P('branch', 'dp')
- copy_expand_weight: bfloat16 [2048, 8192], P('dp', 'branch')
- copy_shrink_weight: bfloat16 [8192, 2048], P('branch', 'dp')
Inputs may be any that keep to these rules, and one draw needn't show every extreme that they name: `segments`: in every row the document numbers start at 0, never fall from token to token; each document holds 1 to 448 tokens, and one document in each row holds exactly 448.
All inputs are finite; a program needn't handle non-finite values.
Results may differ from a plain program's by a relative error of at most 0.012.
The roundings to bfloat16 on the way count: a program that leaves them out, or rounds other values in their place, can miss the bound.
Values may be sent and summed in bfloat16 or wider, within the bound.
A program may use at most 256 MiB of HBM per device.

v0:
```python
import math

import jax
import jax.numpy as jnp
from jax import lax
from jax.sharding import PartitionSpec as P

D = 2048
HEAD_DIM = 64
ROT = 32
FF = 8192
STEP = 3


EPS_NORM = 1e-05
ROPE_BASE = 10000.0
BETA_ONE = 0.5
BETA_TWO = 0.5
ADAM_EPS = 1e-08
DECAY = 0.1
MATRIX_RATE = 0.03
VECTOR_RATE = 0.3
MASKED = -1e30


def gelu_tanh(value):
    return (
        0.5
        * value
        * (1.0 + jnp.tanh(0.7978845608028654 * (value + 0.044715 * value * value * value)))
    )


def doc_positions(segments):
    length = segments.shape[-1]
    places = jnp.arange(length, dtype=jnp.int32)
    before = jnp.concatenate([segments[..., :1] - 1, segments[..., :-1]], axis=-1)
    starts = jnp.where(segments != before, places, 0)
    starts = lax.cummax(starts, axis=segments.ndim - 1)
    return places - starts


def rotary_tables(positions):
    half = ROT // 2
    freq = ROPE_BASE ** (-(jnp.arange(half, dtype=jnp.float32) * 2.0) / ROT)
    angle = positions.astype(jnp.float32)[..., None] * freq
    return (jnp.cos(angle), jnp.sin(angle))


def rotate(values, cosine, sine):
    half = ROT // 2
    first = values[..., :half]
    second = values[..., half:ROT]
    cosine = cosine[..., None, :]
    sine = sine[..., None, :]
    return jnp.concatenate(
        [first * cosine - second * sine, second * cosine + first * sine, values[..., ROT:]], axis=-1
    )


def block_scores(query_rows, keys, allowed, scale):
    scores = (
        jnp.einsum("qhe,khe->hqk", query_rows, keys, preferred_element_type=jnp.float32) * scale
    )
    return jnp.where(allowed[None], scores, MASKED)


def adamw(weight, grad, first, second, rate, decay, count):
    first_new = BETA_ONE * first + (1.0 - BETA_ONE) * grad
    second_new = BETA_TWO * second + (1.0 - BETA_TWO) * grad * grad
    first_fix = 1.0 - BETA_ONE**count
    second_fix = 1.0 - BETA_TWO**count
    update = first_new / first_fix / (jnp.sqrt(second_new / second_fix) + ADAM_EPS)
    return (weight - rate * (update + decay * weight), first_new, second_new)


def on_device(
    inputs,
    segments,
    out_grad,
    layer_params,
    attend_weight,
    attend_bias,
    output_weight,
    expand_weight,
    expand_bias,
    shrink_weight,
    mean_layer,
    mean_attend_weight,
    mean_attend_bias,
    mean_output_weight,
    mean_expand_weight,
    mean_expand_bias,
    mean_shrink_weight,
    square_layer,
    square_attend_weight,
    square_attend_bias,
    square_output_weight,
    square_expand_weight,
    square_expand_bias,
    square_shrink_weight,
):
    attend_low, output_low, expand_low, shrink_low, bias_attend, bias_expand = (
        lax.all_gather(attend_weight.astype(jnp.bfloat16), "dp", axis=1, tiled=True),
        lax.all_gather(output_weight.astype(jnp.bfloat16), "dp", axis=1, tiled=True),
        lax.all_gather(expand_weight.astype(jnp.bfloat16), "dp", axis=0, tiled=True),
        lax.all_gather(shrink_weight.astype(jnp.bfloat16), "dp", axis=1, tiled=True),
        lax.all_gather(attend_bias.astype(jnp.bfloat16), "dp", axis=1, tiled=True),
        lax.all_gather(expand_bias.astype(jnp.bfloat16), "dp", axis=0, tiled=True),
    )
    width = attend_low.shape[2]
    heads_here = width // HEAD_DIM
    micro = inputs.shape[0]
    scale = HEAD_DIM ** (-0.5)
    gain = layer_params[0]
    shift = layer_params[1]
    results = []
    input_grads = []
    small_total = jnp.zeros((3, layer_params.shape[1]), jnp.float32)
    reduced = None
    gathered = None
    for index in range(micro):
        rows = inputs[index].astype(jnp.float32)
        center = rows - jnp.mean(rows, -1, keepdims=True)
        inverse = lax.rsqrt(jnp.mean(center * center, -1, keepdims=True) + EPS_NORM)
        normal = center * inverse
        whole = lax.all_gather(
            (normal * gain + shift).astype(jnp.bfloat16), "branch", axis=0, tiled=True
        )
        length = whole.shape[0]
        seg_row = segments[index]
        cosine, sine = rotary_tables(doc_positions(seg_row))
        places = jnp.arange(length, dtype=jnp.int32)
        allowed = (places[None, :] <= places[:, None]) & (seg_row[:, None] == seg_row[None, :])
        proj = jnp.einsum("ld,cde->cle", whole, attend_low, preferred_element_type=jnp.float32)
        proj = proj + bias_attend.astype(jnp.float32)[:, None, :]
        split = proj.reshape(3, length, heads_here, HEAD_DIM)
        query = rotate(split[0], cosine, sine).astype(jnp.bfloat16)
        keys = rotate(split[1], cosine, sine).astype(jnp.bfloat16)
        values = split[2].astype(jnp.bfloat16)
        block = min(length, 512)
        scores = block_scores(query, keys, allowed, scale)
        top = jnp.max(scores, -1, keepdims=True)
        expo = jnp.exp(scores - top)
        total = jnp.sum(expo, -1, keepdims=True)
        probs_low = (expo / total).astype(jnp.bfloat16)
        contexts = jnp.einsum("hqk,khe->qhe", probs_low, values, preferred_element_type=jnp.float32)
        log_totals = [top + jnp.log(total)]
        context = contexts.reshape(length, width).astype(jnp.bfloat16)
        up = jnp.dot(whole, expand_low, preferred_element_type=jnp.float32) + bias_expand.astype(
            jnp.float32
        )
        act = gelu_tanh(up).astype(jnp.bfloat16)
        partial_out = jnp.dot(context, output_low, preferred_element_type=jnp.float32)
        partial_out = partial_out + jnp.dot(act, shrink_low, preferred_element_type=jnp.float32)
        summed = lax.psum_scatter(partial_out, "branch", scatter_dimension=0, tiled=True)
        result = (rows + summed + layer_params[2]).astype(jnp.bfloat16)
        grad_here = out_grad[index]
        grad_whole = lax.all_gather(grad_here, "branch", axis=0, tiled=True)
        grad_output = jnp.einsum(
            "le,ld->ed", context, grad_whole, preferred_element_type=jnp.float32
        )
        grad_shrink = jnp.einsum("lf,ld->fd", act, grad_whole, preferred_element_type=jnp.float32)
        d_context = jnp.einsum(
            "ld,ed->le", grad_whole, output_low, preferred_element_type=jnp.float32
        ).astype(jnp.bfloat16)
        d_act = jnp.einsum("ld,fd->lf", grad_whole, shrink_low, preferred_element_type=jnp.float32)
        gelu_value, gelu_pull = jax.vjp(gelu_tanh, up)
        d_up = gelu_pull(d_act)[0].astype(jnp.bfloat16)
        grad_expand = jnp.einsum("ld,lf->df", whole, d_up, preferred_element_type=jnp.float32)
        grad_expand_bias = jnp.sum(d_up.astype(jnp.float32), 0)
        d_heads = d_context.reshape(length, heads_here, HEAD_DIM)
        key_grad = jnp.zeros((length, heads_here, HEAD_DIM), jnp.float32)
        value_grad = jnp.zeros((length, heads_here, HEAD_DIM), jnp.float32)
        query_grads = []
        for number, start in enumerate(range(0, length, block)):
            scores = block_scores(query, keys, allowed, scale)
            probs = jnp.exp(scores - log_totals[number])
            probs_low = probs.astype(jnp.bfloat16)
            value_grad = jnp.einsum(
                "hqk,qhe->khe", probs_low, d_heads, preferred_element_type=jnp.float32
            )
            d_probs = jnp.einsum(
                "qhe,khe->hqk", d_heads, values, preferred_element_type=jnp.float32
            )
            d_scores = (probs * (d_probs - jnp.sum(probs * d_probs, -1, keepdims=True))).astype(
                jnp.bfloat16
            )
            query_grads.append(
                jnp.einsum("hqk,khe->qhe", d_scores, keys, preferred_element_type=jnp.float32)
                * scale
            )
            key_grad = (
                jnp.einsum("hqk,qhe->khe", d_scores, query, preferred_element_type=jnp.float32)
                * scale
            )
        d_query = rotate(query_grads[0], cosine, -sine).astype(jnp.bfloat16)
        d_key = rotate(key_grad, cosine, -sine).astype(jnp.bfloat16)
        d_value = value_grad.astype(jnp.bfloat16)
        d_proj = jnp.stack([d_query, d_key, d_value]).reshape(3, length, width)
        grad_attend = jnp.einsum("ld,cle->cde", whole, d_proj, preferred_element_type=jnp.float32)
        grad_attend_bias = jnp.sum(d_proj.astype(jnp.float32), 1)
        d_whole = jnp.einsum("cle,cde->ld", d_proj, attend_low, preferred_element_type=jnp.float32)
        d_whole = d_whole + jnp.einsum(
            "lf,df->ld", d_up, expand_low, preferred_element_type=jnp.float32
        )
        d_normed = lax.psum_scatter(d_whole, "branch", scatter_dimension=0, tiled=True)
        grad_gain = jnp.sum(d_normed * normal, 0)
        grad_shift = jnp.sum(d_normed, 0)
        d_normal = d_normed * gain
        d_rows = inverse * (
            d_normal
            - jnp.mean(d_normal, -1, keepdims=True)
            - normal * jnp.mean(d_normal * normal, -1, keepdims=True)
        )
        d_rows = (d_rows + grad_here.astype(jnp.float32)).astype(jnp.bfloat16)
        small = jnp.stack([grad_gain, grad_shift, jnp.sum(grad_here.astype(jnp.float32), 0)])
        local = (
            grad_attend,
            grad_output,
            grad_expand,
            grad_shrink,
            grad_attend_bias,
            grad_expand_bias,
        )
        result, d_rows, small, local = (result, d_rows, small, local)
        results.append(result)
        input_grads.append(d_rows)
        small_total = small_total + small
        gathered = local if gathered is None else jax.tree.map(jnp.add, gathered, local)
    reduced = (
        lax.psum_scatter(gathered[0], "dp", scatter_dimension=1, tiled=True),
        lax.psum_scatter(gathered[1], "dp", scatter_dimension=1, tiled=True),
        lax.psum_scatter(gathered[2], "dp", scatter_dimension=0, tiled=True),
        lax.psum_scatter(gathered[3], "dp", scatter_dimension=1, tiled=True),
        lax.psum_scatter(gathered[4], "dp", scatter_dimension=1, tiled=True),
        lax.psum_scatter(gathered[5], "dp", scatter_dimension=0, tiled=True),
    )
    squares = sum((jnp.sum(piece * piece) for piece in reduced))
    small_sum, square_sum = lax.psum((small_total, squares), ("dp", "branch"))
    norm_value = jnp.sqrt(square_sum + jnp.sum(small_sum * small_sum))
    factor = jnp.minimum(1.0, math.sqrt(4 * D * D + 2 * D * FF) / norm_value)
    count = float(STEP)
    params = (
        layer_params,
        attend_weight,
        attend_bias,
        output_weight,
        expand_weight,
        expand_bias,
        shrink_weight,
    )
    grads = (small_sum, reduced[0], reduced[4], reduced[1], reduced[2], reduced[5], reduced[3])
    firsts = (
        mean_layer,
        mean_attend_weight,
        mean_attend_bias,
        mean_output_weight,
        mean_expand_weight,
        mean_expand_bias,
        mean_shrink_weight,
    )
    seconds = (
        square_layer,
        square_attend_weight,
        square_attend_bias,
        square_output_weight,
        square_expand_weight,
        square_expand_bias,
        square_shrink_weight,
    )
    is_matrix = (False, True, False, True, True, False, True)
    weights_new, firsts_new, seconds_new = ([], [], [])
    for weight, grad, first, second, matrix in zip(params, grads, firsts, seconds, is_matrix):
        rate = MATRIX_RATE if matrix else VECTOR_RATE
        decay = DECAY if matrix else 0.0
        weight_new, first_new, second_new = adamw(
            weight, factor * grad, first, second, rate, decay, count
        )
        weights_new.append(weight_new)
        firsts_new.append(first_new)
        seconds_new.append(second_new)
    return (
        jnp.stack(results, 0),
        jnp.stack(input_grads, 0),
        norm_value.reshape(1),
        weights_new[0],
        weights_new[1],
        weights_new[2],
        weights_new[3],
        weights_new[4],
        weights_new[5],
        weights_new[6],
        firsts_new[0],
        firsts_new[1],
        firsts_new[2],
        firsts_new[3],
        firsts_new[4],
        firsts_new[5],
        firsts_new[6],
        seconds_new[0],
        seconds_new[1],
        seconds_new[2],
        seconds_new[3],
        seconds_new[4],
        seconds_new[5],
        seconds_new[6],
        weights_new[1].astype(jnp.bfloat16),
        weights_new[3].astype(jnp.bfloat16),
        weights_new[4].astype(jnp.bfloat16),
        weights_new[6].astype(jnp.bfloat16),
    )


def solution(mesh):
    return jax.shard_map(
        on_device,
        mesh=mesh,
        in_specs=(
            P("dp", "branch", None),
            P("dp", None),
            P("dp", "branch", None),
            P(),
            P(None, "dp", "branch"),
            P(None, ("branch", "dp")),
            P("branch", "dp"),
            P("dp", "branch"),
            P(("branch", "dp")),
            P("branch", "dp"),
            P(),
            P(None, "dp", "branch"),
            P(None, ("branch", "dp")),
            P("branch", "dp"),
            P("dp", "branch"),
            P(("branch", "dp")),
            P("branch", "dp"),
            P(),
            P(None, "dp", "branch"),
            P(None, ("branch", "dp")),
            P("branch", "dp"),
            P("dp", "branch"),
            P(("branch", "dp")),
            P("branch", "dp"),
        ),
        out_specs=(
            P("dp", "branch", None),
            P("dp", "branch", None),
            P(),
            P(),
            P(None, "dp", "branch"),
            P(None, ("branch", "dp")),
            P("branch", "dp"),
            P("dp", "branch"),
            P(("branch", "dp")),
            P("branch", "dp"),
            P(),
            P(None, "dp", "branch"),
            P(None, ("branch", "dp")),
            P("branch", "dp"),
            P("dp", "branch"),
            P(("branch", "dp")),
            P("branch", "dp"),
            P(),
            P(None, "dp", "branch"),
            P(None, ("branch", "dp")),
            P("branch", "dp"),
            P("dp", "branch"),
            P(("branch", "dp")),
            P("branch", "dp"),
            P(None, "dp", "branch"),
            P("branch", "dp"),
            P("dp", "branch"),
            P("branch", "dp"),
        ),
        check_vma=False,
    )
```

profile of v0, /device:TPU:0, one launch (start us, length us, event | category | flops | bytes accessed | tf_op | source)
XLA Modules:
  0.0 1729.0 jit_solution(16702037341180618674)
XLA Ops:
  26.4 22.1 %all-gather.2 = bf16[8,64,3]{1,2,0:T(4,128)(2,1)S(1)} all-gather(bf16[1,64,3]{1,2,0:T(4,128)(2,1)S(1)} %convert_bitcast_fusion.4), channel_id=1, replica_groups=mesh['dp'=8,'branch'=4] {'dp'}, dimensions={0}, use_global_device_ids=true | all-gather | bytes 3456 | tf_op jit(solution)/shard_map/all_gather | solution.py:108
  51.4 37.8 %all-gather.17.cloned.1.call-done = bf16[512,2048]{1,0:T(8,128)(2,1)} async-done(((bf16[512,256]{1,0:T(8,128)(2,1)}), bf16[512,2048]{1,0:T(8,128)(2,1)}) %all-gather.17.cloned.1.call-update) | async-done | bytes 2097168 | tf_op jit(solution)/shard_map/all_gather | solution.py:105
  89.3 4.4 fusion.67
  93.7 18.5 %all-gather.25.cloned.1.call-done = bf16[1,512,2048]{2,1,0:T(8,128)(2,1)} async-done(((bf16[1,128,2048]{2,1,0:T(8,128)(2,1)}), bf16[1,512,2048]{2,1,0:T(8,128)(2,1)}) %all-gather.25.cloned.1.call-update) | async-done | bytes 2097168 | tf_op jit(solution)/shard_map/all_gather | solution.py:159
  115.1 21.7 %all-gather.23.cloned.1.call-done = bf16[512,2048]{1,0:T(8,128)(2,1)} async-done(((bf16[128,2048]{1,0:T(8,128)(2,1)}), bf16[512,2048]{1,0:T(8,128)(2,1)}) %all-gather.23.cloned.1.call-update) | async-done | bytes 2097168 | tf_op jit(solution)/shard_map/all_gather | solution.py:127
  136.8 102.4 %all-gather.15.cloned.1.call-done = bf16[3,2048,512]{1,2,0:T(8,128)(2,1)} async-done(((bf16[3,256,512]{1,2,0:T(8,128)(2,1)}), bf16[3,2048,512]{1,2,0:T(8,128)(2,1)}) %all-gather.15.cloned.1.call-update) | async-done | bytes 6291472 | tf_op jit(solution)/shard_map/all_gather | solution.py:104
  239.3 6.4 add_bitcast_fusion.1
  247.5 14.6 all-gather.13.cloned.1.call-done
  262.1 6.2 add_bitcast_fusion.2
  279.0 5.5 multiply_reduce_fusion.1
  304.6 5.4 multiply_reduce_fusion
  319.3 5.8 fusion.71
  325.1 5.8 fusion.70
  334.2 3.3 convolution_add_fusion.2
  338.2 20.7 %all-gather.3 = bf16[8,1,256]{2,1,0:T(2,128)(2,1)S(1)} all-gather(bf16[1,1,256]{2,1,0:T(2,128)(2,1)S(1)} %reshape.538), channel_id=1, replica_groups=mesh['dp'=8,'branch'=4] {'dp'}, dimensions={0}, use_global_device_ids=true | all-gather | bytes 4608 | tf_op jit(solution)/shard_map/all_gather | solution.py:109
  358.9 31.1 %all-gather.19.cloned.1.call-done = bf16[2048,2048]{1,0:T(8,128)(2,1)} async-done(((bf16[256,2048]{1,0:T(8,128)(2,1)}), bf16[2048,2048]{1,0:T(8,128)(2,1)}) %all-gather.19.cloned.1.call-update) | async-done | bytes 8388624 | tf_op jit(solution)/shard_map/all_gather | solution.py:106
  390.0 10.5 fusion.170
  400.5 115.6 %all-gather.21.cloned.1.call-done = bf16[2048,2048]{1,0:T(8,128)(2,1)} async-done(((bf16[2048,256]{1,0:T(8,128)(2,1)}), bf16[2048,2048]{1,0:T(8,128)(2,1)}) %all-gather.21.cloned.1.call-update) | async-done | bytes 8388624 | tf_op jit(solution)/shard_map/all_gather | solution.py:107
  516.1 9.6 fusion.148
  525.7 3.4 convolution_add_fusion.4
  530.7 11.4 convert_reduce_fusion.1
  542.1 7.8 fusion.172
  549.9 7.9 bitcast_add_fusion.1
  559.4 7.0 fusion.171
  566.5 9.3 fusion.149
  575.9 3.4 convolution_add_fusion.3
  579.3 11.4 convert_reduce_fusion
  590.7 7.7 fusion.173
  598.5 7.9 bitcast_add_fusion
  606.5 5.7 fusion.47
  612.2 6.9 add_bitcast_fusion
  619.2 7.0 fusion.174
  626.2 13.1 convolution_add_fusion.1
  639.5 14.4 fusion.34
  653.9 12.2 convolution_add_fusion
  675.4 18.9 %all-reduce = f32[2048]{0:T(1024)S(1)} all-reduce(f32[2048]{0:T(1024)S(1)} %add.391), channel_id=13, replica_groups=mesh['dp'=8,'branch'=4] {'dp'}, use_global_device_ids=true, to_apply=%region_36.37.clone | all-reduce | flops 2048 | bytes 16384
  696.7 20.7 %reduce-scatter.12.cloned.1.call-done = f32[128,2048]{1,0:T(8,128)} async-done(((f32[512,2048]{1,0:T(8,128)}), f32[128,2048]{1,0:T(8,128)}) %reduce-scatter.12.cloned.1.call-update) | async-done | bytes 1048592 | tf_op jit(solution)/shard_map/reduce_scatter | solution.py:156
  717.4 46.9 %reduce-scatter.16.cloned.1.call-done = f32[128,2048]{1,0:T(8,128)} async-done(((f32[512,2048]{1,0:T(8,128)}), f32[128,2048]{1,0:T(8,128)}) %reduce-scatter.16.cloned.1.call-update) | async-done | bytes 1048592 | tf_op jit(solution)/shard_map/reduce_scatter | solution.py:207
  764.3 47.2 %reduce-scatter.14.cloned.1.call-done = f32[128,2048]{1,0:T(8,128)} async-done(((f32[512,2048]{1,0:T(8,128)}), f32[128,2048]{1,0:T(8,128)}) %reduce-scatter.14.cloned.1.call-update) | async-done | bytes 1048592 | tf_op jit(solution)/shard_map/reduce_scatter | solution.py:156
  811.5 46.9 %reduce-scatter.18.cloned.1.call-done = f32[128,2048]{1,0:T(8,128)} async-done(((f32[512,2048]{1,0:T(8,128)}), f32[128,2048]{1,0:T(8,128)}) %reduce-scatter.18.cloned.1.call-update) | async-done | bytes 1048592 | tf_op jit(solution)/shard_map/reduce_scatter | solution.py:207
  858.5 4.1 fusion.106
  864.7 205.4 %reduce-scatter.20.cloned.1.call-done = f32[3,256,512]{1,2,0:T(8,128)} async-done(((f32[3,2048,512]{1,2,0:T(8,128)}), f32[3,256,512]{1,2,0:T(8,128)}) %reduce-scatter.20.cloned.1.call-update) | async-done | bytes 1572880 | tf_op jit(solution)/shard_map/reduce_scatter | solution.py:232
  1074.0 282.0 %reduce-scatter.24.cloned.1.call-done = f32[256,2048]{1,0:T(8,128)} async-done(((f32[2048,2048]{1,0:T(8,128)}), f32[256,2048]{1,0:T(8,128)}) %reduce-scatter.24.cloned.1.call-update) | async-done | bytes 2097168 | tf_op jit(solution)/shard_map/reduce_scatter | solution.py:234
  1359.4 282.1 %reduce-scatter.26.cloned.1.call-done = f32[2048,256]{1,0:T(8,128)} async-done(((f32[2048,2048]{1,0:T(8,128)}), f32[2048,256]{1,0:T(8,128)}) %reduce-scatter.26.cloned.1.call-update) | async-done | bytes 2097168 | tf_op jit(solution)/shard_map/reduce_scatter | solution.py:235
  1648.4 39.5 %all-reduce.1 = (f32[]{:T(128)}, f32[3,2048]{1,0:T(4,128)S(1)}) all-reduce(f32[]{:T(128)S(6)} %add.392, f32[3,2048]{1,0:T(4,128)S(1)} %maximum_add_fusion), channel_id=1, replica_groups=mesh['dp'=8,'branch'=4] {'dp','branch'}, use_global_device_ids=true, to_apply=%region_38.39 | all-reduce | flops 6145 | bytes 49160 | tf_op jit(solution)/shard_map/psum | solution.py:240
  1689.9 5.2 fusion.156
  1710.3 6.6 fusion.150
  1716.9 4.2 fusion.152
  (353 shorter events, 111.3 us)
Async XLA Ops:
  7.2 8.1 copy-start.43
  7.2 44.2 %all-gather.27.cloned.1.call-start = ((), (), s32[]{:S(2)}) async-start(), calls=%async_computation.24 | async-start | bytes 2621440 | tf_op jit(solution)/shard_map/all_gather | solution.py:159
  9.7 79.5 %all-gather.17.cloned.1.call-start = ((), (), s32[]{:S(2)}) async-start(), calls=%async_computation.11 | async-start | bytes 2359296 | tf_op jit(solution)/shard_map/all_gather | solution.py:105
  11.6 100.6 %all-gather.25.cloned.1.call-start = ((), (), s32[]{:S(2)}) async-start(), calls=%async_computation.23 | async-start | bytes 2621440 | tf_op jit(solution)/shard_map/all_gather | solution.py:159
  12.3 124.5 %all-gather.23.cloned.1.call-start = ((), (), s32[]{:S(2)}) async-start(), calls=%async_computation.15 | async-start | bytes 2621440 | tf_op jit(solution)/shard_map/all_gather | solution.py:127
  15.2 224.0 %all-gather.15.cloned.1.call-start = ((), (), s32[]{:S(2)}) async-start(), calls=%async_computation.10 | async-start | bytes 7077888 | tf_op jit(solution)/shard_map/all_gather | solution.py:104
  16.8 245.2 %all-gather.13.cloned.1.call-start = ((), (), s32[]{:S(2)}) async-start(), calls=%async_computation.9 | async-start | bytes 2621440 | tf_op jit(solution)/shard_map/all_gather | solution.py:127
  17.4 372.6 %all-gather.19.cloned.1.call-start = ((), (), s32[]{:S(2)}) async-start(), calls=%async_computation.12 | async-start | bytes 9437184 | tf_op jit(solution)/shard_map/all_gather | solution.py:106
  20.3 495.8 %all-gather.21.cloned.1.call-start = ((), (), s32[]{:S(2)}) async-start(), calls=%async_computation.13 | async-start | bytes 9437184 | tf_op jit(solution)/shard_map/all_gather | solution.py:107
  23.2 650.7 %reduce-scatter.28.cloned.1.call-start = ((), (), s32[]{:S(2)}) async-start(), calls=%async_computation.25 | async-start | bytes 294912
  89.3 23.0 %copy-start.16 = (bf16[512,2048]{1,0:T(8,128)(2,1)S(1)}, bf16[512,2048]{1,0:T(8,128)(2,1)}, u32[]{:S(2)}) copy-start(bf16[512,2048]{1,0:T(8,128)(2,1)} %all-gather.17.cloned.1.call-done) | copy-start | bytes 6291460
  268.4 10.6 copy-start.40
  316.2 8.9 copy-start.21
  330.9 364.0 %reduce-scatter.22.cloned.1.call-start = ((), (), s32[]{:S(2)}) async-start(), calls=%async_computation.20 | async-start | bytes 4718592 | tf_op jit(solution)/shard_map/reduce_scatter | solution.py:233
  337.5 379.9 %reduce-scatter.12.cloned.1.call-start = ((), (), s32[]{:S(2)}) async-start(), calls=%async_computation.14 | async-start | bytes 5242880 | tf_op jit(solution)/shard_map/reduce_scatter | solution.py:156
  516.1 9.6 copy-start.17
  516.1 9.6 copy-start.28
  529.2 235.2 %reduce-scatter.16.cloned.1.call-start = ((), (), s32[]{:S(2)}) async-start(), calls=%async_computation.17 | async-start | bytes 5242880 | tf_op jit(solution)/shard_map/reduce_scatter | solution.py:207
  557.9 253.7 %reduce-scatter.14.cloned.1.call-start = ((), (), s32[]{:S(2)}) async-start(), calls=%async_computation.16 | async-start | bytes 5242880 | tf_op jit(solution)/shard_map/reduce_scatter | solution.py:156
  566.5 9.3 copy-start.8
  566.5 9.3 copy-start.18
  566.5 9.3 copy-start.25
  579.3 279.2 %reduce-scatter.18.cloned.1.call-start = ((), (), s32[]{:S(2)}) async-start(), calls=%async_computation.18 | async-start | bytes 5242880 | tf_op jit(solution)/shard_map/reduce_scatter | solution.py:207
  606.4 463.7 %reduce-scatter.20.cloned.1.call-start = ((), (), s32[]{:S(2)}) async-start(), calls=%async_computation.19 | async-start | bytes 14155776 | tf_op jit(solution)/shard_map/reduce_scatter | solution.py:232
  619.1 736.8 %reduce-scatter.24.cloned.1.call-start = ((), (), s32[]{:S(2)}) async-start(), calls=%async_computation.21 | async-start | bytes 18874368 | tf_op jit(solution)/shard_map/reduce_scatter | solution.py:234
  639.3 14.6 copy-start.15
  639.3 1002.2 %reduce-scatter.26.cloned.1.call-start = ((), (), s32[]{:S(2)}) async-start(), calls=%async_computation.22 | async-start | bytes 18874368 | tf_op jit(solution)/shard_map/reduce_scatter | solution.py:235
  639.5 14.4 copy-start.9
  666.2 9.2 copy-start.82
  666.2 192.3 %copy-start.3 = (bf16[2,128,2048]{2,1,0:T(8,128)(2,1)S(1)}, bf16[2,128,2048]{2,1,0:T(8,128)(2,1)}, u32[]{:S(2)}) copy-start(bf16[2,128,2048]{2,1,0:T(8,128)(2,1)} %param.24) | copy-start | bytes 3145732
  666.2 192.3 %copy-start.62 = (f32[1,2048]{1,0:T(1,128)S(1)}, f32[1,2048]{1,0:T(1,128)}, u32[]{:S(2)}) copy-start(f32[1,2048]{1,0:T(1,128)} %copy-done.61) | copy-start | bytes 24580
  666.2 192.3 %copy-start.74 = (f32[1,2048]{1,0:T(1,128)S(1)}, f32[1,2048]{1,0:T(1,128)}, u32[]{:S(2)}) copy-start(f32[1,2048]{1,0:T(1,128)} %get-tuple-element.221) | copy-start | bytes 24580
  666.2 192.3 %copy-start.79 = (f32[128]{0:T(128)S(1)}, f32[128]{0:T(128)}, u32[]{:S(2)}) copy-start(f32[128]{0:T(128)} %copy-done.78) | copy-start | bytes 1540
  666.2 192.3 %copy-start.81 = (f32[128]{0:T(128)S(1)}, f32[128]{0:T(128)}, u32[]{:S(2)}) copy-start(f32[128]{0:T(128)} %copy-done.80) | copy-start | bytes 1540
  666.2 192.3 %copy-start.86 = (f32[128]{0:T(128)S(1)}, f32[128]{0:T(128)}, u32[]{:S(2)}) copy-start(f32[128]{0:T(128)} %copy-done.85) | copy-start | bytes 1540
  666.2 192.3 %copy-start.88 = (f32[128]{0:T(128)S(1)}, f32[128]{0:T(128)}, u32[]{:S(2)}) copy-start(f32[128]{0:T(128)} %copy-done.87) | copy-start | bytes 1540
  764.3 98.3 %copy-start.26 = (f32[128,2048]{1,0:T(8,128)S(1)}, f32[128,2048]{1,0:T(8,128)}, u32[]{:S(2)}) copy-start(f32[128,2048]{1,0:T(8,128)} %reduce-scatter.16.cloned.1.call-done) | copy-start | bytes 3145732
  864.7 825.2 %copy-start.5 = (f32[3,256,512]{1,2,0:T(8,128)S(1)}, f32[3,256,512]{1,2,0:T(8,128)}, u32[]{:S(2)}) copy-start(f32[3,256,512]{1,2,0:T(8,128)} %copy-done.4) | copy-start | bytes 4718596
  1070.1 619.8 %copy-start.19 = (f32[3,256,512]{1,2,0:T(8,128)S(1)}, f32[3,256,512]{1,2,0:T(8,128)}, u32[]{:S(2)}) copy-start(f32[3,256,512]{1,2,0:T(8,128)} %reduce-scatter.20.cloned.1.call-done) | copy-start | bytes 4718596
  1697.6 8.0 copy-start.94
  1697.6 8.7 copy-start.84
  1697.6 8.7 copy-start.89
  1697.6 8.7 copy-start.90
  1697.6 9.3 copy-start.67
  1697.6 9.3 copy-start.75
  1697.6 9.2 copy-start.76
  1697.7 9.9 copy-start.33
  1697.7 9.9 copy-start.34
  (70 other events, 284.9 us)
Sparse Core Ops, SparseCore 0:
  10.2 25.2 all-gather.26
  38.1 51.0 all-gather.16
  91.4 20.7 all-gather.24
  114.2 22.5 all-gather.22
  139.3 99.9 all-gather.14
  241.2 20.7 all-gather.12
  264.8 125.2 all-gather.18
  392.6 123.4 all-gather.20
  520.0 59.3 reduce-scatter.27
  582.9 87.4 reduce-scatter.21
  673.1 44.2 reduce-scatter.11
  719.8 44.4 reduce-scatter.15
  767.0 44.4 reduce-scatter.13
  813.9 44.4 reduce-scatter.17
  862.3 207.7 reduce-scatter.19
  1074.2 281.6 reduce-scatter.23
  1359.6 281.8 reduce-scatter.25
where the time goes:
time: 1740 us; the launch traced here: 1730 us
  waiting for transfers between devices  1270 us (73%)
  matrix products  218 us (13%)
  blocking collectives  101 us (6%)
  other arithmetic  69.4 us (4%)
  local copies, waits for them, and re-layouts  41.4 us (2%)
  between operations  24.1 us (1%)
    reduce_scatter x1, waiting for transfers between devices, on_device(): lax.psum_scatter(gathered[3], 'dp', scatter_dimension=1, tiled=True)  282 us
    reduce_scatter x1, waiting for transfers between devices, on_device(): lax.psum_scatter(gathered[2], 'dp', scatter_dimension=0, tiled=True)  282 us
    reduce_scatter x1, waiting for transfers between devices, on_device(): lax.psum_scatter(gathered[0], 'dp', scatter_dimension=1, tiled=True)  205 us
    all_gather x1, waiting for transfers between devices, on_device(): lax.all_gather(shrink_weight.astype(jnp.bfloat16), 'dp', axis=1, tiled=True)  116 us
    all_gather x1, waiting for transfers between devices, on_device(): lax.all_gather(attend_weight.astype(jnp.bfloat16), 'dp', axis=1, tiled=True)  102 us
    reduce_scatter x2, waiting for transfers between devices, on_device(): lax.psum_scatter(d_whole, 'branch', scatter_dimension=0, tiled=True)  93.8 us
    reduce_scatter x2, waiting for transfers between devices, on_device(): lax.psum_scatter(partial_out, 'branch', scatter_dimension=0, tiled=True)  67.9 us
    psum x1, blocking collectives, on_device(): small_sum, square_sum = lax.psum((small_total, squares), ('dp', 'branch'))  39.5 us
  transfers between devices with their start and end apart: 17, of which 14 were waited for; matrix products, arithmetic and copies ran while one was open for 16% of the time, Pallas kernels for 0%

commit v1 on v0

v1 whole, which is shorter than its diff:
```python
import math

import jax
import jax.numpy as jnp
from jax import lax
from jax.experimental import pallas as pl
from jax.experimental.pallas import tpu as pltpu
from jax.sharding import PartitionSpec as P

HEAD_DIM = 64
ROT = 32
STEP = 3

EPS_NORM = 1e-05
ROPE_BASE = 10000.0
BETA_ONE = 0.5
BETA_TWO = 0.5
ADAM_EPS = 1e-08
DECAY = 0.1
MATRIX_RATE = 0.03
VECTOR_RATE = 0.3
MASKED = -1e30

AXES = ("dp", "branch")
LOW = jnp.bfloat16
F32 = jnp.float32


def doc_positions(segments):
    length = segments.shape[-1]
    places = jnp.arange(length, dtype=jnp.int32)
    before = jnp.concatenate([segments[..., :1] - 1, segments[..., :-1]], axis=-1)
    starts = jnp.where(segments != before, places, 0)
    starts = lax.cummax(starts, axis=segments.ndim - 1)
    return places - starts


def rotary_lanes(positions):
    half = ROT // 2
    lane = jnp.arange(2 * HEAD_DIM, dtype=jnp.int32) % HEAD_DIM
    freq = ROPE_BASE ** (-((lane % half).astype(F32) * 2.0) / ROT)
    angle = positions.astype(F32)[..., None] * freq
    cosine = jnp.where(lane < ROT, jnp.cos(angle), 1.0)
    sine = jnp.sin(angle)
    up = jnp.where(lane < half, -sine, 0.0)
    down = jnp.where((lane >= half) & (lane < ROT), sine, 0.0)
    return cosine, up, down


def gelu_parts(up):
    inner = 0.7978845608028654 * (up + 0.044715 * up * up * up)
    t = jnp.tanh(inner)
    value = 0.5 * up * (1.0 + t)
    slope = 0.5 * (1.0 + t) + 0.5 * up * (1.0 - t * t) * 0.7978845608028654 * (
        1.0 + 3.0 * 0.044715 * up * up
    )
    return value, slope


def dot(a, b, dims, out=F32):
    return lax.dot_general(a, b, (dims, ((), ())), preferred_element_type=F32).astype(out)


def attention_kernel(q_ref, k_ref, v_ref, d_ref, cos_ref, up_ref, down_ref, segc_ref, segr_ref,
                     ctx_ref, dq_ref, dk_ref, dv_ref, dk_acc, dv_acc):
    length, lanes = q_ref.shape
    half = ROT // 2
    block = length // 2
    scale = HEAD_DIM ** (-0.5)
    cosine, up, down = cos_ref[...], up_ref[...], down_ref[...]

    def rot(x, sign):
        return (x * cosine + sign * (pltpu.roll(x, lanes - half, 1) * up + pltpu.roll(x, half, 1) * down))

    q = rot(q_ref[...], 1.0).astype(LOW)
    k = rot(k_ref[...], 1.0).astype(LOW)
    v = v_ref[...].astype(LOW)
    d = d_ref[...]
    lane = lax.broadcasted_iota(jnp.int32, (length, lanes), 1)
    dk_acc[...] = jnp.zeros_like(dk_acc)
    dv_acc[...] = jnp.zeros_like(dv_acc)
    for i in range(2):
        keys = (i + 1) * block
        rows = slice(i * block, (i + 1) * block)
        place_q = lax.broadcasted_iota(jnp.int32, (block, keys), 0) + i * block
        place_k = lax.broadcasted_iota(jnp.int32, (block, keys), 1)
        allowed = (place_k <= place_q) & (segc_ref[rows, :] == segr_ref[:, :keys])
        ctx = jnp.zeros((block, lanes), F32)
        dq = jnp.zeros((block, lanes), F32)
        for h in range(lanes // HEAD_DIM):
            mine = lane // HEAD_DIM == h
            zero = jnp.zeros((), LOW)
            qm = jnp.where(mine[rows], q[rows], zero)
            dm = jnp.where(mine[rows], d[rows], zero)
            km = jnp.where(mine[:keys], k[:keys], zero)
            vm = jnp.where(mine[:keys], v[:keys], zero)
            s = dot(qm, k[:keys], ((1,), (1,))) * scale
            s = jnp.where(allowed, s, MASKED)
            e = jnp.exp(s - jnp.max(s, -1, keepdims=True))
            p = e * (1.0 / jnp.sum(e, -1, keepdims=True))
            p_low = p.astype(LOW)
            ctx = ctx + dot(p_low, vm, ((1,), (0,)))
            dp = dot(dm, v[:keys], ((1,), (1,)))
            ds = (p * (dp - jnp.sum(p * dp, -1, keepdims=True))).astype(LOW)
            dq = dq + dot(ds, km, ((1,), (0,)))
            dk_acc[:keys, :] += dot(ds, qm, ((0,), (0,)))
            dv_acc[:keys, :] += dot(p_low, dm, ((0,), (0,)))
        ctx_ref[rows, :] = ctx.astype(LOW)
        dq = dq * scale
        dq_ref[rows, :] = (
            dq * cosine[rows]
            - (pltpu.roll(dq, lanes - half, 1) * up[rows] + pltpu.roll(dq, half, 1) * down[rows])
        ).astype(LOW)
    dk_ref[...] = rot(dk_acc[...] * scale, -1.0).astype(LOW)
    dv_ref[...] = dv_acc[...].astype(LOW)


def attention(proj, d_context, segments):
    rows, length = segments.shape
    width = d_context.shape[1]
    pair = 2 * HEAD_DIM
    pairs = width // pair
    cosine, up, down = rotary_lanes(doc_positions(segments).reshape(rows * length))
    part = lambda c: pl.BlockSpec((length, pair), lambda r, h: (r, c * pairs + h))
    table = pl.BlockSpec((length, pair), lambda r, h: (r, 0))
    out = jax.ShapeDtypeStruct((rows * length, width), LOW)
    return pl.pallas_call(
        attention_kernel,
        grid=(rows, pairs),
        in_specs=[
            part(0), part(1), part(2), part(0), table, table, table,
            pl.BlockSpec((length, 1), lambda r, h: (r, 0)),
            pl.BlockSpec((None, 1, length), lambda r, h: (r, 0, 0)),
        ],
        out_specs=[part(0)] * 4,
        out_shape=[out] * 4,
        scratch_shapes=[pltpu.VMEM((length, pair), F32)] * 2,
        cost_estimate=pl.CostEstimate(
            flops=14 * rows * length * length * width,
            bytes_accessed=rows * length * width * 24,
            transcendentals=rows * length * length * width // HEAD_DIM,
        ),
    )(proj, proj, proj, d_context, cosine, up, down,
      segments.reshape(rows * length, 1), segments.reshape(rows, 1, length))


class Place:
    def __init__(self, nd, nb):
        self.nz, self.nb = nd // 2, nb
        dp, branch = lax.axis_index("dp"), lax.axis_index("branch")
        self.dp, self.branch = dp, branch
        self.z, self.x = dp // 2, dp % 2
        self.y, self.c = branch // 2, branch % 2

    def send(self, value, to):
        pairs = []
        for z in range(self.nz):
            for x in range(2):
                for b in range(self.nb):
                    t = to(z, x, b // 2, b % 2)
                    if t is not None:
                        pairs.append(((2 * z + x) * self.nb + b, (2 * t[0] + t[1]) * self.nb + 2 * t[2] + t[3]))
        return lax.ppermute(value, AXES, perm=pairs)

    def swap_x(self, v):
        return self.send(v, lambda z, x, y, c: (z, 1 - x, y, c))

    def swap_c(self, v):
        return self.send(v, lambda z, x, y, c: (z, x, y, 1 - c))

    def swap_first(self, v):
        return self.send(v, lambda z, x, y, c: (z, 1 - x, y, c) if c == 0 else (z, x, 1 - y, c))

    def swap_second(self, v):
        return self.send(v, lambda z, x, y, c: (z, x, 1 - y, c) if c == 0 else (z, 1 - x, y, c))

    def along_z(self, v, hops):
        return self.send(v, lambda z, x, y, c: (hops[z], x, y, c) if z in hops else None)


def gather_tokens(at, own):
    rows, block, d = own.shape
    first = at.swap_first(own)
    second = at.swap_second(own)
    third = at.swap_second(first)
    pieces = [own, first, second, third]
    full = jnp.zeros((2, rows, at.nb, block, d), own.dtype)
    c0 = at.c == 0
    flips = [(0, 0), (jnp.where(c0, 1, 0), jnp.where(c0, 0, 1)), (jnp.where(c0, 0, 1), jnp.where(c0, 1, 0)), (1, 1)]
    for piece, (fx, fy) in zip(pieces, flips):
        for other in (0, 1):
            here = at.swap_c(piece) if other else piece
            if other:
                gx, gy = (fy, fx)
            else:
                gx, gy = (fx, fy)
            spot = (at.x + gx) % 2, 2 * ((at.y + gy) % 2) + (at.c + other) % 2
            full = lax.dynamic_update_slice(
                full, here[None, :, None], (spot[0], 0, spot[1], 0, 0))
    return full


def scatter_tokens(at, part):
    _, rows, nb, block, d = part.shape
    part = part.reshape(2, rows, 2, 2, block, d)
    pick = lambda v, i, axis: lax.dynamic_index_in_dim(v, i, axis, keepdims=False)
    got = at.swap_c(pick(part, 1 - at.c, 3))
    p = pick(part, at.c, 3).astype(F32) + got.astype(F32)
    c0 = at.c == 0
    by_y = lambda v, i: pick(v, i, 2)
    by_x = lambda v, i: jnp.moveaxis(pick(v, i, 0), 1, 0)
    got = at.swap_second(jnp.where(c0, by_y(p, 1 - at.y), by_x(p, 1 - at.x)).astype(LOW))
    q = jnp.where(c0, by_y(p, at.y), by_x(p, at.x)) + got.astype(F32)
    i = jnp.where(c0, at.x, at.y)
    got = at.swap_first(pick(q, 1 - i, 0).astype(LOW))
    return pick(q, i, 0) + got.astype(F32)


def gather_z(at, chunk):
    if at.nz == 4:
        odd = at.z % 2 == 1
        got = at.along_z(chunk, {0: 1, 1: 0, 2: 3, 3: 2})
        two = jnp.where(odd, jnp.concatenate([got, chunk]), jnp.concatenate([chunk, got]))
        near = at.along_z(two, {1: 2, 2: 1})
        far = at.along_z(near, {1: 0, 2: 3})
        rest = jnp.where((at.z == 1) | (at.z == 2), near, far)
        return jnp.where(at.z < 2, jnp.concatenate([two, rest]), jnp.concatenate([rest, two]))
    n, cols = chunk.shape
    full = jnp.zeros((at.nz * n, cols), chunk.dtype)
    ring = {z: (z + 1) % at.nz for z in range(at.nz)}
    for step in range(at.nz):
        full = lax.dynamic_update_slice(full, chunk, (((at.z - step) % at.nz) * n, 0))
        if step < at.nz - 1:
            chunk = at.along_z(chunk, ring)
    return full


def scatter_z(at, part):
    n = part.shape[0] // at.nz
    part = part.reshape(at.nz, n, part.shape[1])
    pick = lambda v, i: lax.dynamic_index_in_dim(v, i, 0, keepdims=False)
    if at.nz == 4:
        half = at.z // 2
        mine = lax.dynamic_slice_in_dim(part, 2 * half, 2, 0)
        away = lax.dynamic_slice_in_dim(part, 2 - 2 * half, 2, 0)
        got = at.along_z(away, {0: 1, 3: 2})
        got = at.along_z((away.astype(F32) + got.astype(F32)).astype(LOW), {1: 2, 2: 1})
        total = mine.astype(F32) + got.astype(F32)
        got = at.along_z(pick(total, 1 - at.z % 2).astype(LOW), {0: 1, 1: 0, 2: 3, 3: 2})
        return pick(total, at.z % 2) + got.astype(F32)
    ring = {z: (z + 1) % at.nz for z in range(at.nz)}
    total = pick(part, (at.z - 1) % at.nz).astype(F32)
    for step in range(1, at.nz):
        got = at.along_z(total.astype(LOW), ring)
        total = pick(part, (at.z - 1 - step) % at.nz).astype(F32) + got.astype(F32)
    return total


def adamw(weight, grad, first, second, rate, decay, count):
    first_new = BETA_ONE * first + (1.0 - BETA_ONE) * grad
    second_new = BETA_TWO * second + (1.0 - BETA_TWO) * grad * grad
    first_fix = 1.0 - BETA_ONE**count
    second_fix = 1.0 - BETA_TWO**count
    update = first_new / first_fix / (jnp.sqrt(second_new / second_fix) + ADAM_EPS)
    return (weight - rate * (update + decay * weight), first_new, second_new)


def on_device(
    nd,
    nb,
    inputs,
    segments,
    out_grad,
    layer_params,
    attend_weight,
    attend_bias,
    output_weight,
    expand_weight,
    expand_bias,
    shrink_weight,
    mean_layer,
    mean_attend_weight,
    mean_attend_bias,
    mean_output_weight,
    mean_expand_weight,
    mean_expand_bias,
    mean_shrink_weight,
    square_layer,
    square_attend_weight,
    square_attend_bias,
    square_output_weight,
    square_expand_weight,
    square_expand_bias,
    square_shrink_weight,
):
    at = Place(nd, nb)
    x0 = at.x == 0
    rows, block, d = inputs.shape
    length = segments.shape[1]
    tokens = 2 * rows * length
    heads2 = attend_weight.shape[2] // 2
    hidden2 = expand_weight.shape[1] // 2
    gain, shift, out_bias = layer_params[0], layer_params[1], layer_params[2]

    data = inputs.astype(F32)
    center = data - jnp.mean(data, -1, keepdims=True)
    inverse = lax.rsqrt(jnp.mean(center * center, -1, keepdims=True) + EPS_NORM)
    normal = center * inverse
    normed = (normal * gain + shift).astype(LOW)

    def halves(h):
        cols = lambda w: lax.dynamic_slice_in_dim(w, h * heads2, heads2, w.ndim - 1)
        att = attend_weight.astype(LOW)
        attend = jnp.concatenate(
            [cols(att[0]), cols(att[1]), cols(att[2]),
             lax.dynamic_slice_in_dim(output_weight.astype(LOW), h * heads2, heads2, 0).T], 1)
        expand = lax.dynamic_slice_in_dim(expand_weight.astype(LOW), h * hidden2, hidden2, 1)
        shrink = lax.dynamic_slice_in_dim(shrink_weight.astype(LOW), h * hidden2, hidden2, 0).T
        return attend, expand, shrink

    whole = []
    for mine, theirs in zip(halves(at.x), halves(1 - at.x)):
        got = at.swap_x(theirs)
        chunk = jnp.where(x0, jnp.concatenate([mine, got]), jnp.concatenate([got, mine]))
        whole.append(gather_z(at, chunk))
    attend, expand, shrink = whole
    biases = jnp.concatenate([attend_bias.reshape(-1), expand_bias]).astype(LOW)
    biases = lax.all_gather(biases, "dp", axis=0)
    n_att = attend_bias.shape[1]
    bias_att = jnp.moveaxis(biases[:, : 3 * n_att].reshape(nd, 3, n_att), 0, 1).reshape(3, -1)
    bias_att = lax.dynamic_slice_in_dim(bias_att, at.x * heads2, heads2, 1).astype(F32)
    bias_exp = lax.dynamic_slice_in_dim(
        biases[:, 3 * n_att:].reshape(-1), at.x * hidden2, hidden2, 0).astype(F32)

    tok = gather_tokens(at, normed).reshape(tokens, d)
    dy = gather_tokens(at, out_grad).reshape(tokens, d)
    got = at.swap_x(segments)
    segs = jnp.where(x0, jnp.concatenate([segments, got]), jnp.concatenate([got, segments]))

    att_w, wo_t = attend[:, : 3 * heads2], attend[:, 3 * heads2:]
    proj = dot(tok, att_w, ((1,), (0,))) + bias_att.reshape(-1)
    d_context = dot(dy, wo_t, ((1,), (0,)), LOW)
    context, d_query, d_key, d_value = attention(proj, d_context, segs)
    d_proj = jnp.concatenate([d_query, d_key, d_value], 1)

    up = dot(tok, expand, ((1,), (0,))) + bias_exp
    act, slope = gelu_parts(up)
    act = act.astype(LOW)
    d_up = (dot(dy, shrink, ((1,), (0,))) * slope).astype(LOW)

    grad_attend = jnp.concatenate(
        [dot(tok, d_proj, ((0,), (0,)), LOW), dot(dy, context, ((0,), (0,)), LOW)], 1)
    grad_shrink = dot(dy, act, ((0,), (0,)), LOW)
    grad_expand = dot(tok, d_up, ((0,), (0,)), LOW)

    def owned(part):
        total = scatter_z(at, part)
        total = total.reshape(2, total.shape[0] // 2, total.shape[1])
        pick = lambda i: lax.dynamic_index_in_dim(total, i, 0, keepdims=False)
        mine = pick(at.x)
        got = at.swap_x(pick(1 - at.x).astype(LOW)).astype(F32)
        return jnp.where(x0, mine, got), jnp.where(x0, got, mine)

    lo_a, hi_a = owned(grad_attend)
    lo_s, hi_s = owned(grad_shrink)
    lo_e, hi_e = owned(grad_expand)
    join = lambda i: jnp.concatenate(
        [lo_a[:, i * heads2:(i + 1) * heads2], hi_a[:, i * heads2:(i + 1) * heads2]], 1)
    g_attend = jnp.stack([join(0), join(1), join(2)])
    g_output = join(3).T
    g_expand = jnp.concatenate([lo_e, hi_e], 1)
    g_shrink = jnp.concatenate([lo_s, hi_s], 1).T

    partial = dot(act, shrink, ((1,), (1,))) + dot(context, wo_t, ((1,), (1,)))
    partial = partial.astype(LOW).reshape(2, rows, nb, block, d)
    summed = scatter_tokens(at, partial)
    result = (data + summed + out_bias).astype(LOW)

    partial = dot(d_up, expand, ((1,), (1,))) + dot(d_proj, att_w, ((1,), (1,)))
    partial = partial.astype(LOW).reshape(2, rows, nb, block, d)
    d_normed = scatter_tokens(at, partial)
    grad_gain = jnp.sum(d_normed * normal, (0, 1))
    grad_shift = jnp.sum(d_normed, (0, 1))
    d_normal = d_normed * gain
    d_rows = inverse * (
        d_normal
        - jnp.mean(d_normal, -1, keepdims=True)
        - normal * jnp.mean(d_normal * normal, -1, keepdims=True)
    )
    back = out_grad.astype(F32)
    d_rows = (d_rows + back).astype(LOW)

    sum_att = jnp.sum(d_proj.astype(F32), 0).reshape(3, heads2)
    sum_exp = jnp.sum(d_up.astype(F32), 0)
    spread_att = lax.dynamic_update_slice(jnp.zeros((3, 2 * heads2), F32), sum_att, (0, at.x * heads2))
    spread_exp = lax.dynamic_update_slice(jnp.zeros((2 * hidden2,), F32), sum_exp, (at.x * hidden2,))
    spread = lax.psum(jnp.concatenate([spread_att.reshape(-1), spread_exp]), "dp")
    n_exp = expand_bias.shape[0]
    g_bias_att = lax.dynamic_slice_in_dim(
        spread[: 6 * heads2].reshape(3, 2 * heads2), at.dp * n_att, n_att, 1)
    g_bias_exp = lax.dynamic_slice_in_dim(spread[6 * heads2:], at.dp * n_exp, n_exp, 0)

    small = jnp.stack([grad_gain, grad_shift, jnp.sum(back, (0, 1))])
    pieces = (lo_a, hi_a, lo_s, hi_s, lo_e, hi_e, g_bias_att, g_bias_exp)
    squares = sum(jnp.sum(piece * piece) for piece in pieces)
    g_small, squares = lax.psum((small, squares), AXES)
    norm_value = jnp.sqrt(squares + jnp.sum(g_small * g_small))
    size = 4 * d * d + 2 * d * 2 * hidden2 * nb
    factor = jnp.minimum(1.0, math.sqrt(size) / norm_value)
    count = float(STEP)
    params = (layer_params, attend_weight, attend_bias, output_weight, expand_weight, expand_bias, shrink_weight)
    grads = (g_small, g_attend, g_bias_att, g_output, g_expand, g_bias_exp, g_shrink)
    firsts = (mean_layer, mean_attend_weight, mean_attend_bias, mean_output_weight, mean_expand_weight,
              mean_expand_bias, mean_shrink_weight)
    seconds = (square_layer, square_attend_weight, square_attend_bias, square_output_weight,
               square_expand_weight, square_expand_bias, square_shrink_weight)
    is_matrix = (False, True, False, True, True, False, True)
    weights_new, firsts_new, seconds_new = ([], [], [])
    for weight, grad, first, second, matrix in zip(params, grads, firsts, seconds, is_matrix):
        rate = MATRIX_RATE if matrix else VECTOR_RATE
        decay = DECAY if matrix else 0.0
        new = adamw(weight, factor * grad, first, second, rate, decay, count)
        weights_new.append(new[0])
        firsts_new.append(new[1])
        seconds_new.append(new[2])
    return (
        result,
        d_rows,
        norm_value.reshape(1),
        *weights_new,
        *firsts_new,
        *seconds_new,
        weights_new[1].astype(LOW),
        weights_new[3].astype(LOW),
        weights_new[4].astype(LOW),
        weights_new[6].astype(LOW),
    )


def solution(mesh):
    nd, nb = mesh.shape["dp"], mesh.shape["branch"]
    state = (
        P(),
        P(None, "dp", "branch"),
        P(None, ("branch", "dp")),
        P("branch", "dp"),
        P("dp", "branch"),
        P(("branch", "dp")),
        P("branch", "dp"),
    )
    rows = P("dp", "branch", None)
    return jax.shard_map(
        lambda *args: on_device(nd, nb, *args),
        mesh=mesh,
        in_specs=(rows, P("dp", None), rows) + state * 3,
        out_specs=(rows, rows, P()) + state * 3 + (state[1], state[3], state[4], state[6]),
        check_vma=False,
    )
```

time: 1740 us -> 974 us (0.56)
  waiting for transfers between devices: 1270 us -> 193 us
  starting transfers between devices: 0.87 us -> 163 us
  blocking collectives: 101 us -> 195 us
  matrix products: 218 us -> 152 us
  local copies, waits for them, and re-layouts: 41.4 us -> 99.8 us
  other arithmetic: 69.4 us -> 120 us
  Pallas kernels: 0 us -> 30.8 us
    reduce_scatter x8 -> x0, waiting for transfers between devices: 931 us -> none  [the longest x1 282 us: on_device(): lax.psum_scatter(gathered[3], 'dp', scatter_dimension=1, tiled=True)]
    all_gather x8 -> x0, waiting for transfers between devices: 342 us -> none  [the longest x1 116 us: on_device(): lax.all_gather(shrink_weight.astype(jnp.bfloat16), 'dp', axis=1, tiled=True)]
    ppermute x0 -> x45, waiting for transfers between devices: none -> 193 us  [send(): return lax.ppermute(value, AXES, perm=pairs)]
    ppermute x0 -> x45, starting transfers between devices: none -> 163 us  [send(): return lax.ppermute(value, AXES, perm=pairs)]
    psum x1 -> x2, blocking collectives: 39.5 us -> 163 us  [the longest x1 115 us: on_device(): lax.psum(jnp.concatenate([spread_att.reshape(-1), spread_exp]), 'dp')]
    dot_general x36 -> x12, matrix products: 218 us -> 152 us  [dot(): lax.dot_general(a, b, (dims, ((), ())), preferred_element_type=F32)]
    pallas_call x0 -> x1, Pallas kernels: none -> 30.8 us  [attention(): pl.pallas_call(attention_kernel, grid=(rows, pairs), in_specs=[part(0), p...]
    add x5 -> x11, other arithmetic: 0.08 us -> 30.1 us  [the longest x2 10.7 us: scatter_tokens(): p = pick(part, at.c, 3).astype(F32) + got.astype(F32)]
  transfers between devices with their start and end apart: 17 -> 45, of which waited for: 14 -> 12; matrix products, arithmetic and copies ran while one was open for 16% -> 28% of each run, Pallas kernels for 0% -> 3%
where the time goes in v1:
time: 974 us; the launch traced here: 964 us
  blocking collectives  195 us (20%)
  waiting for transfers between devices  193 us (20%)
  starting transfers between devices  163 us (17%)
  matrix products  152 us (16%)
  other arithmetic  120 us (12%)
  local copies, waits for them, and re-layouts  99.8 us (10%)
  Pallas kernels  30.8 us (3%)
  between operations  9.77 us (1%)
    ppermute x45, waiting for transfers between devices, send(): return lax.ppermute(value, AXES, perm=pairs)  193 us
    ppermute x45, starting transfers between devices, send(): return lax.ppermute(value, AXES, perm=pairs)  163 us
    dot_general x12, matrix products, dot(): lax.dot_general(a, b, (dims, ((), ())), preferred_element_type=F32)  152 us
    psum x1, blocking collectives, on_device(): lax.psum(jnp.concatenate([spread_att.reshape(-1), spread_exp]), 'dp')  115 us
    psum x1, blocking collectives, on_device(): g_small, squares = lax.psum((small, squares), AXES)  47.7 us
    unnamed x154, local copies, waits for them, and re-layouts  44.5 us
    all_gather x1, blocking collectives, on_device(): biases = lax.all_gather(biases, 'dp', axis=0)  32 us
    pallas_call x1, Pallas kernels, attention(): pl.pallas_call(attention_kernel, grid=(rows, pairs), in_specs=[part(0), p...  30.8 us
  transfers between devices with their start and end apart: 45, of which 12 were waited for; matrix products, arithmetic and copies ran while one was open for 28% of the time, Pallas kernels for 3%

profile of v1, /device:TPU:0, one launch (start us, length us, event | category | flops | bytes accessed | tf_op | source)
XLA Modules:
  0.0 963.8 jit_solution(785177778610995612)
XLA Ops:
  11.9 3.3 copy-done.14
  21.4 32.0 %all-gather = bf16[8,1,448]{2,1,0:T(2,128)(2,1)S(1)} all-gather(bf16[1,1,448]{2,1,0:T(2,128)(2,1)S(1)} %maximum_bitcast_fusion.3), channel_id=1, replica_groups=mesh['dp'=8,'branch'=4] {'dp'}, dimensions={0}, use_global_device_ids=true | all-gather | bytes 8064 | tf_op jit(solution)/shard_map/all_gather | solution.py:328
  53.5 4.3 broadcast.218.clone.1
  67.8 6.5 fusion.34
  91.1 8.4 collective-permute-done.20
  100.5 10.2 %collective-permute-done.1 = bf16[2,128,2048]{2,1,0:T(8,128)(2,1)S(1)} collective-permute-done((bf16[2,128,2048]{2,1,0:T(8,128)(2,1)}, bf16[2,128,2048]{2,1,0:T(8,128)(2,1)S(1)}, u32[]{:S(2)}, u32[]{:S(2)}) %collective-permute-start.1) | collective-permute-done | bytes 1048608 | tf_op jit(solution)/shard_map/ppermute | solution.py:163
  112.9 20.1 %collective-permute-done.8 = bf16[512,1024]{0,1:T(8,128)(2,1)S(1)} collective-permute-done((bf16[512,1024]{0,1:T(8,128)(2,1)S(1)}, bf16[512,1024]{0,1:T(8,128)(2,1)S(1)}, u32[]{:S(2)}, u32[]{:S(2)}) %collective-permute-start.8) | collective-permute-done | bytes 1048608 | tf_op jit(solution)/shard_map/ppermute | solution.py:163
  134.3 13.7 %collective-permute-done.12 = bf16[512,1024]{0,1:T(8,128)(2,1)S(1)} collective-permute-done((bf16[512,1024]{0,1:T(8,128)(2,1)S(1)}, bf16[512,1024]{0,1:T(8,128)(2,1)S(1)}, u32[]{:S(2)}, u32[]{:S(2)}) %collective-permute-start.12) | collective-permute-done | bytes 1048608 | tf_op jit(solution)/shard_map/ppermute | solution.py:163
  157.8 8.6 collective-permute-done.5
  173.1 72.6 %collective-permute-done.18 = bf16[1024,1024]{0,1:T(8,128)(2,1)S(1)} collective-permute-done((bf16[1024,1024]{0,1:T(8,128)(2,1)S(1)}, bf16[1024,1024]{0,1:T(8,128)(2,1)S(1)}, u32[]{:S(2)}, u32[]{:S(2)}) %collective-permute-start.18) | collective-permute-done | bytes 2097184 | tf_op jit(solution)/shard_map/ppermute | solution.py:163
  247.6 8.3 convolution_convert_fusion.4.d_ref
  255.9 8.6 broadcast_add_fusion.q_ref.k_ref.v_ref
  264.5 26.1 %collective-permute-done.10 = bf16[1024,1024]{0,1:T(8,128)(2,1)S(1)} collective-permute-done((bf16[1024,1024]{0,1:T(8,128)(2,1)S(1)}, bf16[1024,1024]{0,1:T(8,128)(2,1)S(1)}, u32[]{:S(2)}, u32[]{:S(2)}) %collective-permute-start.10) | collective-permute-done | bytes 2097184 | tf_op jit(solution)/shard_map/ppermute | solution.py:163
  290.8 11.7 %fusion.46 = f32[2048,1024]{1,0:T(8,128)} fusion(bf16[2048,2048]{1,0:T(8,128)(2,1)S(1)} %bitcast.242, bf16[1024,1024]{0,1:T(8,128)(2,1)S(1)} %broadcast_select_fusion.2, bf16[1024,1024]{0,1:T(8,128)(2,1)S(1)} %maximum_select_fusion.3, pred[]{:T(512)S(6)} %lt.344), kind=kOutput, calls=%fused_computation.149 | convolution fusion | flops 8608808960 | bytes 20971520 | tf_op jit(solution)/shard_map/dot_general | solution.py:61
  302.6 30.8 %shard_map.447 = (bf16[2048,256]{1,0:T(8,128)(2,1)}, bf16[2048,256]{1,0:T(8,128)(2,1)}, bf16[2048,256]{1,0:T(8,128)(2,1)}, bf16[2048,256]{1,0:T(8,128)(2,1)}) custom-call(f32[2048,768]{1,0:T(8,128)} %broadcast_add_fusion.q_ref.k_ref.v_ref, f32[2048,768]{1,0:T(8,128)} %broadcast_add_fusion.q_ref.k_ref.v_ref, f32[2048,768]{1,0:T(8,128)} %broadcast_add_fusion.q_ref.k_ref.v_ref, ...), custom_call_target="tpu_custom_call" | custom-call | flops 3758096384 | bytes 12582912 | tf_op jit(solution)/shard_map/pallas_call | solution.py:127
  337.5 9.5 fusion.11
  347.0 6.9 convolution_convert_fusion.3
  353.9 8.1 fusion.43
  362.0 7.7 convolution_convert_fusion.2
  373.1 19.6 %convert_reduce_fusion = (f32[1024]{0:T(1024)S(1)}, bf16[2048,1024]{1,0:T(8,128)(2,1)}) fusion(f32[2048,1024]{1,0:T(8,128)} %fusion.46, f32[1024]{0:T(1024)S(1)} %copy-done.58, bf16[2048,2048]{1,0:T(8,128)(2,1)} %bitcast.42, bf16[1024,1024]{0,1:T(8,128)(2,1)S(1)} %broadcast_select_fusion.1, bf16[1024,1024]{0,1:T(8,128)(2,1)S(1)} %copy-done.34, pred[]{:T(512)S(6)} %lt.344), kind=kOutput, calls=%fused_computation.13 | convolution fusion | flops 8654945280 | bytes 25174016 | tf_op jit(solution)/shard_map/dot_general | solution.py:61
  392.7 23.1 %add_convert_fusion.1 = bf16[2048,2048]{1,0:T(8,128)(2,1)} fusion(f32[2048,2048]{1,0:T(8,128)} %fusion.43, bf16[1024,1024]{0,1:T(8,128)(2,1)} %copy-done.28, bf16[1024,1024]{0,1:T(8,128)(2,1)} %copy-done.33, pred[]{:T(512)S(6)} %lt.344, f32[2048,1024]{1,0:T(8,128)} %fusion.46, f32[1024]{0:T(1024)S(1)} %copy-done.58), kind=kOutput, calls=%fused_computation.1 | convolution fusion | flops 8638169088 | bytes 37752832 | tf_op jit(solution)/shard_map/dot_general | solution.py:61
  415.8 4.9 dynamic-slice_bitcast_fusion.1
  420.8 13.2 %convolution_convert_fusion = bf16[2048,1024]{1,0:T(8,128)(2,1)} fusion(bf16[2048,2048]{1,0:T(8,128)(2,1)} %bitcast.243, bf16[2048,1024]{1,0:T(8,128)(2,1)S(1)} %copy-done.60), kind=kOutput, calls=%fused_computation.36 | convolution fusion | flops 8592031744 | bytes 16777216 | tf_op jit(solution)/shard_map/dot_general | solution.py:61
  433.9 20.7 %add_convert_fusion = bf16[2048,2048]{1,0:T(8,128)(2,1)} fusion(f32[2048,2048]{1,0:T(8,128)} %fusion.11, bf16[2048,1024]{1,0:T(8,128)(2,1)} %get-tuple-element.205, bf16[1024,1024]{0,1:T(8,128)(2,1)} %copy-done.27, bf16[1024,1024]{0,1:T(8,128)(2,1)} %copy-done.32, pred[]{:T(512)S(6)} %lt.344), kind=kOutput, calls=%fused_computation | convolution fusion | flops 8617197568 | bytes 33554432 | tf_op jit(solution)/shard_map/dot_general | solution.py:61
  454.6 4.9 dynamic-slice_bitcast_fusion
  461.5 23.0 %collective-permute-start.41 = (bf16[2,512,1024]{2,1,0:T(8,128)(2,1)}, bf16[2,512,1024]{2,1,0:T(8,128)(2,1)}, u32[]{:S(2)}, u32[]{:S(2)}) collective-permute-start(bf16[2,512,1024]{2,1,0:T(8,128)(2,1)} %constant_dynamic-slice_fusion.1), channel_id=1, source_target_pairs={{0,8},{1,9},{2,10},{3,11},{4,12},{5,13},{6,14},{7,15},{24,16},{25,... | collective-permute-start | bytes 6291464 | tf_op jit(solution)/shard_map/ppermute | solution.py:163
  486.8 6.4 copy.164
  493.2 3.1 constant_dynamic-slice_fusion.3
  498.9 14.8 %convolution_convert_fusion.1 = bf16[2048,1024]{1,0:T(8,128)(2,1)S(1)} fusion(bf16[2048,2048]{1,0:T(8,128)(2,1)} %bitcast.42, f32[2048,1024]{1,0:T(8,128)} %fusion.46, f32[1024]{0:T(1024)S(1)} %copy-done.58), kind=kOutput, calls=%fused_computation.37 | convolution fusion | flops 8613003264 | bytes 20975616 | tf_op jit(solution)/shard_map/dot_general | solution.py:61
  533.6 115.2 %psum.21 = f32[3584]{0:T(1024)S(1)} all-reduce(f32[3584]{0:T(1024)S(1)} %pad_maximum_fusion.3), channel_id=1, replica_groups=mesh['dp'=8,'branch'=4] {'dp'}, use_global_device_ids=true, to_apply=%region_14.15 | all-reduce | flops 3584 | bytes 28672 | tf_op jit(solution)/shard_map/psum | solution.py:397
  650.1 4.5 add_convert_fusion.2
  656.8 3.9 add_convert_fusion.4
  662.6 3.9 add_convert_fusion.3
  668.7 5.4 convert_add_fusion.1
  677.6 5.4 convert_add_fusion
  685.8 66.3 %collective-permute-start.35 = (bf16[512,1024]{1,0:T(8,128)(2,1)S(1)}, bf16[512,1024]{1,0:T(8,128)(2,1)}, u32[]{:S(2)}, u32[]{:S(2)}) collective-permute-start(bf16[512,1024]{1,0:T(8,128)(2,1)S(1)} %fusion.40), channel_id=1, source_target_pairs={{0,8},{1,9},{2,10},{3,11},{4,12},{5,13},{6,14},{7,15},{8,0},{9,1},... | collective-permute-start | bytes 3145736 | tf_op jit(solution)/shard_map/ppermute | solution.py:163
  754.9 3.1 convert_add_fusion.3
  759.2 31.2 %collective-permute-start.39 = (bf16[512,1024]{1,0:T(8,128)(2,1)}, bf16[512,1024]{1,0:T(8,128)(2,1)}, u32[]{:S(2)}, u32[]{:S(2)}) collective-permute-start(bf16[512,1024]{1,0:T(8,128)(2,1)} %fusion.41), channel_id=1, source_target_pairs={{0,8},{1,9},{2,10},{3,11},{4,12},{5,13},{6,14},{7,15},{8,0},{9,1},... | collective-permute-start | bytes 3145736 | tf_op jit(solution)/shard_map/ppermute | solution.py:163
  799.5 6.4 collective-permute-done.39
  812.5 9.3 collective-permute-done.44
  824.1 9.0 collective-permute-done.40
  859.9 6.0 collective-permute-done.29
  866.9 4.3 convert_reduce_fusion.3
  872.2 47.7 %all-reduce = (f32[]{:T(128)}, f32[3,2048]{1,0:T(4,128)S(1)}) all-reduce(f32[]{:T(128)S(6)} %add.712, f32[3,2048]{1,0:T(4,128)S(1)} %pad_maximum_fusion.2), channel_id=1, replica_groups=mesh['dp'=8,'branch'=4] {'dp','branch'}, use_global_device_ids=true, to_apply=%region_17.18 | all-reduce | flops 6145 | bytes 49160 | tf_op jit(solution)/shard_map/psum | solution.py:406
  921.9 7.2 fusion.68
  938.3 3.1 fusion.72
  951.9 7.0 fusion.70
  958.9 3.4 fusion.74
  (360 shorter events, 180.7 us)
Async XLA Ops:
  0.7 83.7 %collective-permute-start.19 = (bf16[2,128,2048]{2,1,0:T(8,128)(2,1)}, bf16[2,128,2048]{2,1,0:T(8,128)(2,1)}, u32[]{:S(2)}, u32[]{:S(2)}) collective-permute-start(bf16[2,128,2048]{2,1,0:T(8,128)(2,1)} %param.26), channel_id=1, source_target_pairs={{0,1},{1,0},{2,3},{3,2},{4,5},{5,4},{6,7},{7,6},{8,9},{9,8},{10,11... | collective-permute-start | bytes 3145736 | tf_op jit(solution)/shard_map/ppermute | solution.py:163
  5.5 72.8 %collective-permute-start.15 = (bf16[256,1024]{0,1:T(8,128)(2,1)}, bf16[256,1024]{0,1:T(8,128)(2,1)}, u32[]{:S(2)}, u32[]{:S(2)}) collective-permute-start(bf16[256,1024]{0,1:T(8,128)(2,1)} %pad_maximum_fusion.1), channel_id=1, source_target_pairs={{0,4},{1,5},{2,6},{3,7},{4,0},{5,1},{6,2},{7,3},{8,12},{9,13},{10,... | collective-permute-start | bytes 1572872 | tf_op jit(solution)/shard_map/ppermute | solution.py:163
  15.2 71.8 %collective-permute-start = (bf16[2,128,2048]{2,1,0:T(8,128)(2,1)}, bf16[2,128,2048]{2,1,0:T(8,128)(2,1)}, u32[]{:S(2)}, u32[]{:S(2)}) collective-permute-start(bf16[2,128,2048]{2,1,0:T(8,128)(2,1)} %get-tuple-element.165), channel_id=1, source_target_pairs={{0,1},{1,0},{2,3},{3,2},{4,5},{5,4},{6,7},{7,6},{8,9},{9,8},{10,11... | collective-permute-start | bytes 3145736 | tf_op jit(solution)/shard_map/ppermute | solution.py:163
  15.4 48.4 %collective-permute-start.26 = (s32[2,512]{1,0:T(2,128)S(1)}, s32[2,512]{1,0:T(2,128)S(1)}, u32[]{:S(2)}, u32[]{:S(2)}) collective-permute-start(s32[2,512]{1,0:T(2,128)S(1)} %copy-done.48), channel_id=1, source_target_pairs={{0,4},{1,5},{2,6},{3,7},{4,0},{5,1},{6,2},{7,3},{8,12},{9,13},{10,... | collective-permute-start | bytes 12296 | tf_op jit(solution)/shard_map/ppermute | solution.py:163
  17.3 58.9 %collective-permute-start.7 = (bf16[256,1024]{0,1:T(8,128)(2,1)}, bf16[256,1024]{0,1:T(8,128)(2,1)}, u32[]{:S(2)}, u32[]{:S(2)}) collective-permute-start(bf16[256,1024]{0,1:T(8,128)(2,1)} %get-tuple-element.184), channel_id=1, source_target_pairs={{0,4},{1,5},{2,6},{3,7},{4,0},{5,1},{6,2},{7,3},{8,12},{9,13},{10,... | collective-permute-start | bytes 1572872 | tf_op jit(solution)/shard_map/ppermute | solution.py:163
  63.8 17.6 %collective-permute-start.11 = (bf16[256,1024]{0,1:T(8,128)(2,1)}, bf16[256,1024]{0,1:T(8,128)(2,1)}, u32[]{:S(2)}, u32[]{:S(2)}) collective-permute-start(bf16[256,1024]{0,1:T(8,128)(2,1)} %get-tuple-element.186), channel_id=1, source_target_pairs={{0,4},{1,5},{2,6},{3,7},{4,0},{5,1},{6,2},{7,3},{8,12},{9,13},{10,... | collective-permute-start | bytes 1572872 | tf_op jit(solution)/shard_map/ppermute | solution.py:163
  76.2 23.2 %collective-permute-start.20 = (bf16[2,128,2048]{2,1,0:T(8,128)(2,1)S(1)}, bf16[2,128,2048]{2,1,0:T(8,128)(2,1)S(1)}, u32[]{:S(2)}, u32[]{:S(2)}) collective-permute-start(bf16[2,128,2048]{2,1,0:T(8,128)(2,1)S(1)} %copy-done.25), channel_id=1, source_target_pairs={{0,4},{1,3},{2,6},{3,1},{4,0},{5,7},{6,2},{7,5},{8,12},{9,11},{10,... | collective-permute-start | bytes 3145736 | tf_op jit(solution)/shard_map/ppermute | solution.py:163
  78.3 55.9 %collective-permute-start.22 = (bf16[2,128,2048]{2,1,0:T(8,128)(2,1)S(1)}, bf16[2,128,2048]{2,1,0:T(8,128)(2,1)S(1)}, u32[]{:S(2)}, u32[]{:S(2)}) collective-permute-start(bf16[2,128,2048]{2,1,0:T(8,128)(2,1)S(1)} %copy-done.25), channel_id=1, source_target_pairs={{0,2},{1,5},{2,0},{3,7},{4,6},{5,1},{6,4},{7,3},{8,10},{9,13},{10,... | collective-permute-start | bytes 3145736 | tf_op jit(solution)/shard_map/ppermute | solution.py:163
  81.4 29.3 %collective-permute-start.1 = (bf16[2,128,2048]{2,1,0:T(8,128)(2,1)}, bf16[2,128,2048]{2,1,0:T(8,128)(2,1)S(1)}, u32[]{:S(2)}, u32[]{:S(2)}) collective-permute-start(bf16[2,128,2048]{2,1,0:T(8,128)(2,1)} %get-tuple-element.165), channel_id=1, source_target_pairs={{0,4},{1,3},{2,6},{3,1},{4,0},{5,7},{6,2},{7,5},{8,12},{9,11},{10,... | collective-permute-start | bytes 3145736 | tf_op jit(solution)/shard_map/ppermute | solution.py:163
  84.4 27.4 %collective-permute-start.16 = (bf16[512,1024]{0,1:T(8,128)(2,1)S(1)}, bf16[512,1024]{0,1:T(8,128)(2,1)S(1)}, u32[]{:S(2)}, u32[]{:S(2)}) collective-permute-start(bf16[512,1024]{0,1:T(8,128)(2,1)S(1)} %maximum_select_fusion.8), channel_id=1, source_target_pairs={{0,8},{1,9},{2,10},{3,11},{4,12},{5,13},{6,14},{7,15},{8,0},{9,1},... | collective-permute-start | bytes 3145736 | tf_op jit(solution)/shard_map/ppermute | solution.py:163
  87.0 46.1 %collective-permute-start.8 = (bf16[512,1024]{0,1:T(8,128)(2,1)S(1)}, bf16[512,1024]{0,1:T(8,128)(2,1)S(1)}, u32[]{:S(2)}, u32[]{:S(2)}) collective-permute-start(bf16[512,1024]{0,1:T(8,128)(2,1)S(1)} %maximum_select_fusion.6), channel_id=1, source_target_pairs={{0,8},{1,9},{2,10},{3,11},{4,12},{5,13},{6,14},{7,15},{8,0},{9,1},... | collective-permute-start | bytes 3145736 | tf_op jit(solution)/shard_map/ppermute | solution.py:163
  99.5 48.5 %collective-permute-start.12 = (bf16[512,1024]{0,1:T(8,128)(2,1)S(1)}, bf16[512,1024]{0,1:T(8,128)(2,1)S(1)}, u32[]{:S(2)}, u32[]{:S(2)}) collective-permute-start(bf16[512,1024]{0,1:T(8,128)(2,1)S(1)} %maximum_select_fusion.7), channel_id=1, source_target_pairs={{0,8},{1,9},{2,10},{3,11},{4,12},{5,13},{6,14},{7,15},{8,0},{9,1},... | collective-permute-start | bytes 3145736 | tf_op jit(solution)/shard_map/ppermute | solution.py:163
  110.7 37.9 %collective-permute-start.21 = (bf16[2,128,2048]{2,1,0:T(8,128)(2,1)S(1)}, bf16[2,128,2048]{2,1,0:T(8,128)(2,1)S(1)}, u32[]{:S(2)}, u32[]{:S(2)}) collective-permute-start(bf16[2,128,2048]{2,1,0:T(8,128)(2,1)S(1)} %collective-permute-done.20), channel_id=1, source_target_pairs={{0,1},{1,0},{2,3},{3,2},{4,5},{5,4},{6,7},{7,6},{8,9},{9,8},{10,11... | collective-permute-start | bytes 3145736 | tf_op jit(solution)/shard_map/ppermute | solution.py:163
  111.8 39.8 %collective-permute-start.3 = (bf16[2,128,2048]{2,1,0:T(8,128)(2,1)}, bf16[2,128,2048]{2,1,0:T(8,128)(2,1)S(1)}, u32[]{:S(2)}, u32[]{:S(2)}) collective-permute-start(bf16[2,128,2048]{2,1,0:T(8,128)(2,1)} %get-tuple-element.165), channel_id=1, source_target_pairs={{0,2},{1,5},{2,0},{3,7},{4,6},{5,1},{6,4},{7,3},{8,10},{9,13},{10,... | collective-permute-start | bytes 3145736 | tf_op jit(solution)/shard_map/ppermute | solution.py:163
  133.0 22.4 %collective-permute-start.24 = (bf16[2,128,2048]{2,1,0:T(8,128)(2,1)S(1)}, bf16[2,128,2048]{2,1,0:T(8,128)(2,1)S(1)}, u32[]{:S(2)}, u32[]{:S(2)}) collective-permute-start(bf16[2,128,2048]{2,1,0:T(8,128)(2,1)S(1)} %collective-permute-done.20), channel_id=1, source_target_pairs={{0,2},{1,5},{2,0},{3,7},{4,6},{5,1},{6,4},{7,3},{8,10},{9,13},{10,... | collective-permute-start | bytes 3145736 | tf_op jit(solution)/shard_map/ppermute | solution.py:163
  134.2 156.6 %copy-start.32 = (bf16[1024,1024]{0,1:T(8,128)(2,1)}, bf16[1024,1024]{0,1:T(8,128)(2,1)S(1)}, u32[]{:S(2)}) copy-start(bf16[1024,1024]{0,1:T(8,128)(2,1)S(1)} %maximum_select_fusion.3) | copy-start | bytes 6291460
  134.2 18.9 %collective-permute-start.2 = (bf16[2,128,2048]{2,1,0:T(8,128)(2,1)S(1)}, bf16[2,128,2048]{2,1,0:T(8,128)(2,1)S(1)}, u32[]{:S(2)}, u32[]{:S(2)}) collective-permute-start(bf16[2,128,2048]{2,1,0:T(8,128)(2,1)S(1)} %collective-permute-done.1), channel_id=1, source_target_pairs={{0,1},{1,0},{2,3},{3,2},{4,5},{5,4},{6,7},{7,6},{8,9},{9,8},{10,11... | collective-permute-start | bytes 3145736 | tf_op jit(solution)/shard_map/ppermute | solution.py:163
  148.0 5.6 collective-permute-start.23
  148.6 17.8 %collective-permute-start.17 = (bf16[1024,1024]{0,1:T(8,128)(2,1)S(1)}, bf16[1024,1024]{0,1:T(8,128)(2,1)S(1)}, u32[]{:S(2)}, u32[]{:S(2)}) collective-permute-start(bf16[1024,1024]{0,1:T(8,128)(2,1)S(1)} %maximum_select_fusion.5), channel_id=1, source_target_pairs={{8,16},{9,17},{10,18},{11,19},{12,20},{13,21},{14,22},{15,23},{16,... | collective-permute-start | bytes 6291464 | tf_op jit(solution)/shard_map/ppermute | solution.py:163
  151.6 14.8 %collective-permute-start.5 = (bf16[2,128,2048]{2,1,0:T(8,128)(2,1)S(1)}, bf16[2,128,2048]{2,1,0:T(8,128)(2,1)S(1)}, u32[]{:S(2)}, u32[]{:S(2)}) collective-permute-start(bf16[2,128,2048]{2,1,0:T(8,128)(2,1)S(1)} %collective-permute-done.1), channel_id=1, source_target_pairs={{0,2},{1,5},{2,0},{3,7},{4,6},{5,1},{6,4},{7,3},{8,10},{9,13},{10,... | collective-permute-start | bytes 3145736 | tf_op jit(solution)/shard_map/ppermute | solution.py:163
  153.2 4.3 collective-permute-start.4
  153.6 16.9 %collective-permute-start.9 = (bf16[1024,1024]{0,1:T(8,128)(2,1)S(1)}, bf16[1024,1024]{0,1:T(8,128)(2,1)S(1)}, u32[]{:S(2)}, u32[]{:S(2)}) collective-permute-start(bf16[1024,1024]{0,1:T(8,128)(2,1)S(1)} %maximum_select_fusion.3), channel_id=1, source_target_pairs={{8,16},{9,17},{10,18},{11,19},{12,20},{13,21},{14,22},{15,23},{16,... | collective-permute-start | bytes 6291464 | tf_op jit(solution)/shard_map/ppermute | solution.py:163
  155.5 16.3 %collective-permute-start.13 = (bf16[1024,1024]{0,1:T(8,128)(2,1)S(1)}, bf16[1024,1024]{0,1:T(8,128)(2,1)}, u32[]{:S(2)}, u32[]{:S(2)}) collective-permute-start(bf16[1024,1024]{0,1:T(8,128)(2,1)S(1)} %maximum_select_fusion.4), channel_id=1, source_target_pairs={{8,16},{9,17},{10,18},{11,19},{12,20},{13,21},{14,22},{15,23},{16,... | collective-permute-start | bytes 6291464 | tf_op jit(solution)/shard_map/ppermute | solution.py:163
  157.5 11.8 %collective-permute-start.25 = (bf16[2,128,2048]{2,1,0:T(8,128)(2,1)S(1)}, bf16[2,128,2048]{2,1,0:T(8,128)(2,1)S(1)}, u32[]{:S(2)}, u32[]{:S(2)}) collective-permute-start(bf16[2,128,2048]{2,1,0:T(8,128)(2,1)S(1)} %collective-permute-done.24), channel_id=1, source_target_pairs={{0,1},{1,0},{2,3},{3,2},{4,5},{5,4},{6,7},{7,6},{8,9},{9,8},{10,11... | collective-permute-start | bytes 3145736 | tf_op jit(solution)/shard_map/ppermute | solution.py:163
  166.4 3.9 collective-permute-start.6
  166.4 79.2 %collective-permute-start.18 = (bf16[1024,1024]{0,1:T(8,128)(2,1)S(1)}, bf16[1024,1024]{0,1:T(8,128)(2,1)S(1)}, u32[]{:S(2)}, u32[]{:S(2)}) collective-permute-start(bf16[1024,1024]{0,1:T(8,128)(2,1)S(1)} %collective-permute-done.17), channel_id=1, source_target_pairs={{8,0},{9,1},{10,2},{11,3},{12,4},{13,5},{14,6},{15,7},{16,24},{17,... | collective-permute-start | bytes 6291464 | tf_op jit(solution)/shard_map/ppermute | solution.py:163
  170.4 120.4 %copy-start.15 = (bf16[2,2,4,128,2048]{4,3,2,1,0:T(8,128)(2,1)}, bf16[2,2,4,128,2048]{4,3,2,1,0:T(8,128)(2,1)S(1)}, u32[]{:S(2)}) copy-start(bf16[2,2,4,128,2048]{4,3,2,1,0:T(8,128)(2,1)S(1)} %bitcast_dynamic-update-slice_fusion.15) | copy-start | bytes 25165828
  170.5 120.1 %collective-permute-start.10 = (bf16[1024,1024]{0,1:T(8,128)(2,1)S(1)}, bf16[1024,1024]{0,1:T(8,128)(2,1)S(1)}, u32[]{:S(2)}, u32[]{:S(2)}) collective-permute-start(bf16[1024,1024]{0,1:T(8,128)(2,1)S(1)} %collective-permute-done.9), channel_id=1, source_target_pairs={{8,0},{9,1},{10,2},{11,3},{12,4},{13,5},{14,6},{15,7},{16,24},{17,... | collective-permute-start | bytes 6291464 | tf_op jit(solution)/shard_map/ppermute | solution.py:163
  171.8 198.0 %collective-permute-start.14 = (bf16[1024,1024]{0,1:T(8,128)(2,1)}, bf16[1024,1024]{0,1:T(8,128)(2,1)}, u32[]{:S(2)}, u32[]{:S(2)}) collective-permute-start(bf16[1024,1024]{0,1:T(8,128)(2,1)} %collective-permute-done.13), channel_id=1, source_target_pairs={{8,0},{9,1},{10,2},{11,3},{12,4},{13,5},{14,6},{15,7},{16,24},{17,... | collective-permute-start | bytes 6291464 | tf_op jit(solution)/shard_map/ppermute | solution.py:163
  420.8 247.9 %collective-permute-start.27 = (bf16[2,2,2,128,2048]{4,3,2,1,0:T(8,128)(2,1)}, bf16[2,2,2,128,2048]{4,3,2,1,0:T(8,128)(2,1)}, u32[]{:S(2)}, u32[]{:S(2)}) collective-permute-start(bf16[2,2,2,128,2048]{4,3,2,1,0:T(8,128)(2,1)} %dynamic-slice_bitcast_fusion.1), channel_id=1, source_target_pairs={{0,1},{1,0},{2,3},{3,2},{4,5},{5,4},{6,7},{7,6},{8,9},{9,8},{10,11... | collective-permute-start | bytes 12582920 | tf_op jit(solution)/shard_map/ppermute | solution.py:163
  459.5 218.1 %collective-permute-start.30 = (bf16[2,2,2,128,2048]{4,3,2,1,0:T(8,128)(2,1)}, bf16[2,2,2,128,2048]{4,3,2,1,0:T(8,128)(2,1)}, u32[]{:S(2)}, u32[]{:S(2)}) collective-permute-start(bf16[2,2,2,128,2048]{4,3,2,1,0:T(8,128)(2,1)} %dynamic-slice_bitcast_fusion), channel_id=1, source_target_pairs={{0,1},{1,0},{2,3},{3,2},{4,5},{5,4},{6,7},{7,6},{8,9},{9,8},{10,11... | collective-permute-start | bytes 12582920 | tf_op jit(solution)/shard_map/ppermute | solution.py:163
  461.5 188.6 %collective-permute-start.41 = (bf16[2,512,1024]{2,1,0:T(8,128)(2,1)}, bf16[2,512,1024]{2,1,0:T(8,128)(2,1)}, u32[]{:S(2)}, u32[]{:S(2)}) collective-permute-start(bf16[2,512,1024]{2,1,0:T(8,128)(2,1)} %constant_dynamic-slice_fusion.1), channel_id=1, source_target_pairs={{0,8},{1,9},{2,10},{3,11},{4,12},{5,13},{6,14},{7,15},{24,16},{25,... | collective-permute-start | bytes 6291464 | tf_op jit(solution)/shard_map/ppermute | solution.py:163
  496.3 160.5 %collective-permute-start.33 = (bf16[2,512,1024]{2,1,0:T(8,128)(2,1)}, bf16[2,512,1024]{2,1,0:T(8,128)(2,1)}, u32[]{:S(2)}, u32[]{:S(2)}) collective-permute-start(bf16[2,512,1024]{2,1,0:T(8,128)(2,1)} %constant_dynamic-slice_fusion.3), channel_id=1, source_target_pairs={{0,8},{1,9},{2,10},{3,11},{4,12},{5,13},{6,14},{7,15},{24,16},{25,... | collective-permute-start | bytes 6291464 | tf_op jit(solution)/shard_map/ppermute | solution.py:163
  517.3 145.3 %collective-permute-start.37 = (bf16[2,512,1024]{2,1,0:T(8,128)(2,1)}, bf16[2,512,1024]{2,1,0:T(8,128)(2,1)}, u32[]{:S(2)}, u32[]{:S(2)}) collective-permute-start(bf16[2,512,1024]{2,1,0:T(8,128)(2,1)} %constant_dynamic-slice_fusion.2), channel_id=1, source_target_pairs={{0,8},{1,9},{2,10},{3,11},{4,12},{5,13},{6,14},{7,15},{24,16},{25,... | collective-permute-start | bytes 6291464 | tf_op jit(solution)/shard_map/ppermute | solution.py:163
  654.7 97.5 %collective-permute-start.42 = (bf16[2,512,1024]{2,1,0:T(8,128)(2,1)}, bf16[2,512,1024]{2,1,0:T(8,128)(2,1)}, u32[]{:S(2)}, u32[]{:S(2)}) collective-permute-start(bf16[2,512,1024]{2,1,0:T(8,128)(2,1)} %add_convert_fusion.2), channel_id=1, source_target_pairs={{8,16},{9,17},{10,18},{11,19},{12,20},{13,21},{14,22},{15,23},{16,... | collective-permute-start | bytes 6291464 | tf_op jit(solution)/shard_map/ppermute | solution.py:163
  660.7 22.3 %collective-permute-start.34 = (bf16[2,512,1024]{2,1,0:T(8,128)(2,1)}, bf16[2,512,1024]{2,1,0:T(8,128)(2,1)}, u32[]{:S(2)}, u32[]{:S(2)}) collective-permute-start(bf16[2,512,1024]{2,1,0:T(8,128)(2,1)} %add_convert_fusion.4), channel_id=1, source_target_pairs={{8,16},{9,17},{10,18},{11,19},{12,20},{13,21},{14,22},{15,23},{16,... | collective-permute-start | bytes 6291464 | tf_op jit(solution)/shard_map/ppermute | solution.py:163
  666.5 88.4 %collective-permute-start.38 = (bf16[2,512,1024]{2,1,0:T(8,128)(2,1)}, bf16[2,512,1024]{2,1,0:T(8,128)(2,1)}, u32[]{:S(2)}, u32[]{:S(2)}) collective-permute-start(bf16[2,512,1024]{2,1,0:T(8,128)(2,1)} %add_convert_fusion.3), channel_id=1, source_target_pairs={{8,16},{9,17},{10,18},{11,19},{12,20},{13,21},{14,22},{15,23},{16,... | collective-permute-start | bytes 6291464 | tf_op jit(solution)/shard_map/ppermute | solution.py:163
  676.0 164.4 %collective-permute-start.28 = (bf16[2,2,128,2048]{3,2,1,0:T(8,128)(2,1)}, bf16[2,2,128,2048]{3,2,1,0:T(8,128)(2,1)}, u32[]{:S(2)}, u32[]{:S(2)}) collective-permute-start(bf16[2,2,128,2048]{3,2,1,0:T(8,128)(2,1)} %fusion.9), channel_id=1, source_target_pairs={{0,2},{1,5},{2,0},{3,7},{4,6},{5,1},{6,4},{7,3},{8,10},{9,13},{10,... | collective-permute-start | bytes 6291464 | tf_op jit(solution)/shard_map/ppermute | solution.py:163
  683.0 69.2 %copy-start.7 = (bf16[2048,1024]{1,0:T(8,128)(2,1)S(1)}, bf16[2048,1024]{1,0:T(8,128)(2,1)}, u32[]{:S(2)}) copy-start(bf16[2048,1024]{1,0:T(8,128)(2,1)} %convolution_convert_fusion) | copy-start | bytes 12582916
  685.8 108.1 %collective-permute-start.35 = (bf16[512,1024]{1,0:T(8,128)(2,1)S(1)}, bf16[512,1024]{1,0:T(8,128)(2,1)}, u32[]{:S(2)}, u32[]{:S(2)}) collective-permute-start(bf16[512,1024]{1,0:T(8,128)(2,1)S(1)} %fusion.40), channel_id=1, source_target_pairs={{0,8},{1,9},{2,10},{3,11},{4,12},{5,13},{6,14},{7,15},{8,0},{9,1},... | collective-permute-start | bytes 3145736 | tf_op jit(solution)/shard_map/ppermute | solution.py:163
  754.8 41.0 %collective-permute-start.43 = (bf16[512,1024]{1,0:T(8,128)(2,1)S(1)}, bf16[512,1024]{1,0:T(8,128)(2,1)}, u32[]{:S(2)}, u32[]{:S(2)}) collective-permute-start(bf16[512,1024]{1,0:T(8,128)(2,1)S(1)} %fusion.42), channel_id=1, source_target_pairs={{0,8},{1,9},{2,10},{3,11},{4,12},{5,13},{6,14},{7,15},{8,0},{9,1},... | collective-permute-start | bytes 3145736 | tf_op jit(solution)/shard_map/ppermute | solution.py:163
  759.2 46.7 %collective-permute-start.39 = (bf16[512,1024]{1,0:T(8,128)(2,1)}, bf16[512,1024]{1,0:T(8,128)(2,1)}, u32[]{:S(2)}, u32[]{:S(2)}) collective-permute-start(bf16[512,1024]{1,0:T(8,128)(2,1)} %fusion.41), channel_id=1, source_target_pairs={{0,8},{1,9},{2,10},{3,11},{4,12},{5,13},{6,14},{7,15},{8,0},{9,1},... | collective-permute-start | bytes 3145736 | tf_op jit(solution)/shard_map/ppermute | solution.py:163
  792.3 43.0 %collective-permute-start.31 = (bf16[2,2,128,2048]{3,2,1,0:T(8,128)(2,1)}, bf16[2,2,128,2048]{3,2,1,0:T(8,128)(2,1)}, u32[]{:S(2)}, u32[]{:S(2)}) collective-permute-start(bf16[2,2,128,2048]{3,2,1,0:T(8,128)(2,1)} %fusion.7), channel_id=1, source_target_pairs={{0,2},{1,5},{2,0},{3,7},{4,6},{5,1},{6,4},{7,3},{8,10},{9,13},{10,... | collective-permute-start | bytes 6291464 | tf_op jit(solution)/shard_map/ppermute | solution.py:163
  795.7 14.9 %collective-permute-start.36 = (bf16[256,1024]{1,0:T(8,128)(2,1)S(1)}, bf16[256,1024]{1,0:T(8,128)(2,1)S(1)}, u32[]{:S(2)}, u32[]{:S(2)}) collective-permute-start(bf16[256,1024]{1,0:T(8,128)(2,1)S(1)} %fusion.48), channel_id=1, source_target_pairs={{0,4},{1,5},{2,6},{3,7},{4,0},{5,1},{6,2},{7,3},{8,12},{9,13},{10,... | collective-permute-start | bytes 1572872 | tf_op jit(solution)/shard_map/ppermute | solution.py:163
  797.5 24.4 %collective-permute-start.44 = (bf16[256,1024]{1,0:T(8,128)(2,1)S(1)}, bf16[256,1024]{1,0:T(8,128)(2,1)S(1)}, u32[]{:S(2)}, u32[]{:S(2)}) collective-permute-start(bf16[256,1024]{1,0:T(8,128)(2,1)S(1)} %fusion.50), channel_id=1, source_target_pairs={{0,4},{1,5},{2,6},{3,7},{4,0},{5,1},{6,2},{7,3},{8,12},{9,13},{10,... | collective-permute-start | bytes 1572872 | tf_op jit(solution)/shard_map/ppermute | solution.py:163
  807.7 25.4 %collective-permute-start.40 = (bf16[256,1024]{1,0:T(8,128)(2,1)S(1)}, bf16[256,1024]{1,0:T(8,128)(2,1)S(1)}, u32[]{:S(2)}, u32[]{:S(2)}) collective-permute-start(bf16[256,1024]{1,0:T(8,128)(2,1)S(1)} %fusion.49), channel_id=1, source_target_pairs={{0,4},{1,5},{2,6},{3,7},{4,0},{5,1},{6,2},{7,3},{8,12},{9,13},{10,... | collective-permute-start | bytes 1572872 | tf_op jit(solution)/shard_map/ppermute | solution.py:163
  839.5 17.3 %collective-permute-start.32 = (bf16[2,128,2048]{2,1,0:T(8,128)(2,1)}, bf16[2,128,2048]{2,1,0:T(8,128)(2,1)}, u32[]{:S(2)}, u32[]{:S(2)}) collective-permute-start(bf16[2,128,2048]{2,1,0:T(8,128)(2,1)} %fusion.39), channel_id=1, source_target_pairs={{0,4},{1,3},{2,6},{3,1},{4,0},{5,7},{6,2},{7,5},{8,12},{9,11},{10,... | collective-permute-start | bytes 3145736 | tf_op jit(solution)/shard_map/ppermute | solution.py:163
  845.5 20.5 %collective-permute-start.29 = (bf16[2,128,2048]{2,1,0:T(8,128)(2,1)S(1)}, bf16[2,128,2048]{2,1,0:T(8,128)(2,1)S(1)}, u32[]{:S(2)}, u32[]{:S(2)}) collective-permute-start(bf16[2,128,2048]{2,1,0:T(8,128)(2,1)S(1)} %fusion.38), channel_id=1, source_target_pairs={{0,4},{1,3},{2,6},{3,1},{4,0},{5,7},{6,2},{7,5},{8,12},{9,11},{10,... | collective-permute-start | bytes 3145736 | tf_op jit(solution)/shard_map/ppermute | solution.py:163
  (62 other events, 594.7 us)

commit v2 on v1

--- a/solution.py
+++ b/solution.py
@@ -1,3 +1,4 @@
+import functools
 import math
 
 import jax
@@ -144,6 +145,263 @@
       segments.reshape(rows * length, 1), segments.reshape(rows, 1, length))
 
 
+MESH = pl.DeviceIdType.MESH
+
+
+def here(nz, nb):
+    dp, branch = lax.axis_index("dp"), lax.axis_index("branch")
+    return dp // 2, dp % 2, branch // 2, branch % 2
+
+
+def head_kernel(nz, nb, nrm, dyo, pack, bias, seg, tok, dy, wts, biases, segs,
+                local, t_send, t_recv, d_send, d_recv, x_send, x_recv, z_send, z_recv, s_send, s_recv):
+    z, x, y, c = here(nz, nb)
+    ident = lambda z, x, y, c: (2 * z + x, 2 * y + c)
+    first = (z, (x + 1 - c) % 2, (y + c) % 2, c)
+    second = (z, (x + c) % 2, (y + 1 - c) % 2, c)
+    sib = (z, x, y, 1 - c)
+    across = (z, 1 - x, y, c)
+
+    barrier = pltpu.get_barrier_semaphore()
+    for t in (across, (z, x, 1 - y, c), sib):
+        pl.semaphore_signal(barrier, inc=1, device_id=ident(*t), device_id_type=MESH)
+
+    @pl.when(z > 0)
+    def _():
+        pl.semaphore_signal(barrier, inc=1, device_id=ident(z - 1, x, y, c), device_id_type=MESH)
+
+    @pl.when(z < nz - 1)
+    def _():
+        pl.semaphore_signal(barrier, inc=1, device_id=ident(z + 1, x, y, c), device_id_type=MESH)
+
+    pl.semaphore_wait(barrier, 3 + jnp.minimum(z, 1) + jnp.minimum(nz - 1 - z, 1))
+
+    def remote(src, dst, send, recv, to):
+        return pltpu.make_async_remote_copy(
+            src_ref=src, dst_ref=dst, send_sem=send, recv_sem=recv, device_id=ident(*to), device_id_type=MESH)
+
+    class Tokens:
+        def __init__(self, src, out, send, recv):
+            self.src, self.out, self.send, self.recv = src, out, send, recv
+
+        def spot(self, dev):
+            return self.out.at[dev[1], :, 2 * dev[2] + dev[3]]
+
+        def copy(self, k):
+            me = (z, x, y, c)
+            opp = (z, 1 - x, 1 - y, c)
+            where, to = [(me, sib), (me, first), (me, second), (first, second), (first, sib), (second, sib), (opp, sib)][k]
+            src = self.src if k < 3 else self.spot(where)
+            return remote(src, self.spot(where), self.send.at[k], self.recv.at[k], to)
+
+    nt, dt = Tokens(nrm, tok, t_send, t_recv), Tokens(dyo, dy, d_send, d_recv)
+
+    def zcopy(k, step, right):
+        origin = z - (step - 1) if right else z + (step - 1)
+        col = x if k == 0 else 1 - x
+        src = wts.at[origin, col]
+        if step == 1 and k == 0:
+            src = pack.at[x]
+        to = (z + 1 if right else z - 1, x, y, c)
+        sem = (k, step - 1, 0 if right else 1)
+        return remote(src, wts.at[origin, col], z_send.at[sem], z_recv.at[sem], to)
+
+    def zsends(step, right):
+        if right:
+            return (z - (step - 1) >= 0) & (z + 1 <= nz - 1)
+        return (z + (step - 1) <= nz - 1) & (z - 1 >= 0)
+
+    def zgets(step, right):
+        return (z - step >= 0) if right else (z + step <= nz - 1)
+
+    def zstart(k, step):
+        for right in (True, False):
+            @pl.when(zsends(step, right))
+            def _():
+                zcopy(k, step, right).start()
+
+    def zarrive(k, step):
+        for right in (True, False):
+            @pl.when(zgets(step, right))
+            def _():
+                zcopy(k, step, right).wait_recv()
+
+    swap = remote(pack.at[1 - x], wts.at[z, x], x_send.at[0], x_recv.at[0], across)
+    own = [
+        pltpu.make_async_copy(nrm, nt.spot((z, x, y, c)), local.at[0]),
+        pltpu.make_async_copy(dyo, dt.spot((z, x, y, c)), local.at[1]),
+        pltpu.make_async_copy(pack.at[x], wts.at[z, x], local.at[2]),
+        pltpu.make_async_copy(bias, biases.at[2 * z + x], local.at[3]),
+        pltpu.make_async_copy(seg, segs.at[x], local.at[4]),
+    ]
+    bias_x = remote(bias, biases.at[2 * z + x], s_send.at[0], s_recv.at[0], across)
+    seg_x = remote(seg, segs.at[x], x_send.at[1], x_recv.at[1], across)
+
+    def bcopy(step, right, k):
+        origin = z - (step - 1) if right else z + (step - 1)
+        row = 2 * origin + (x if k == 0 else 1 - x)
+        sem = 1 + 4 * (step - 1) + 2 * k + (0 if right else 1)
+        to = (z + 1 if right else z - 1, x, y, c)
+        return remote(biases.at[row], biases.at[row], s_send.at[sem], s_recv.at[sem], to)
+
+    swap.start()
+    zstart(0, 1)
+    nt.copy(1).start()
+    nt.copy(2).start()
+    nt.copy(0).start()
+    for copy in own:
+        copy.start()
+    bias_x.start()
+    seg_x.start()
+    own[3].wait()
+    bias_x.wait_recv()
+    swap.wait_recv()
+    zstart(1, 1)
+    for step in range(1, nz):
+        for k in (0, 1):
+            for right in (True, False):
+                @pl.when(zsends(step, right))
+                def _():
+                    bcopy(step, right, k).start()
+        if step == 1:
+            dt.copy(0).start()
+            nt.copy(1).wait_recv()
+            nt.copy(3).start()
+            nt.copy(4).start()
+            dt.copy(1).start()
+            dt.copy(2).start()
+        for k in (0, 1):
+            zarrive(k, step)
+            if step < nz - 1:
+                zstart(k, step + 1)
+        for k in (0, 1):
+            for right in (True, False):
+                @pl.when(zgets(step, right))
+                def _():
+                    bcopy(step, right, k).wait_recv()
+        if step == 1:
+            nt.copy(2).wait_recv()
+            nt.copy(5).start()
+            dt.copy(1).wait_recv()
+            dt.copy(3).start()
+            dt.copy(4).start()
+            nt.copy(3).wait_recv()
+            nt.copy(6).start()
+        if step == min(2, nz - 1):
+            dt.copy(2).wait_recv()
+            dt.copy(5).start()
+            dt.copy(3).wait_recv()
+            dt.copy(6).start()
+    for t in (nt, dt):
+        for k in (0, 4, 5, 6):
+            t.copy(k).wait_recv()
+        for k in range(7):
+            t.copy(k).wait_send()
+    for step in range(1, nz):
+        for k in (0, 1):
+            for right in (True, False):
+                @pl.when(zsends(step, right))
+                def _():
+                    zcopy(k, step, right).wait_send()
+                    bcopy(step, right, k).wait_send()
+    swap.wait_send()
+    bias_x.wait_send()
+    seg_x.wait()
+    for i, copy in enumerate(own):
+        if i != 3:
+            copy.wait()
+
+
+def head(nz, nb, nrm, dyo, pack, bias, seg):
+    rows, block, d = nrm.shape
+    anywhere = pl.BlockSpec(memory_space=pl.ANY)
+    dma = pltpu.SemaphoreType.DMA
+    full = jax.ShapeDtypeStruct((2, rows, nb, block, d), nrm.dtype)
+    return pl.pallas_call(
+        functools.partial(head_kernel, nz, nb),
+        in_specs=[anywhere] * 5,
+        out_specs=[anywhere] * 5,
+        out_shape=[
+            full, full,
+            jax.ShapeDtypeStruct((nz,) + pack.shape, pack.dtype),
+            jax.ShapeDtypeStruct((2 * nz,) + bias.shape, bias.dtype),
+            jax.ShapeDtypeStruct((2,) + seg.shape, seg.dtype),
+        ],
+        scratch_shapes=[
+            dma((5,)), dma((7,)), dma((7,)), dma((7,)), dma((7,)), dma((2,)), dma((2,)),
+            dma((2, nz - 1, 2)), dma((2, nz - 1, 2)), dma((4 * nz,)), dma((4 * nz,)),
+        ],
+        compiler_params=pltpu.CompilerParams(collective_id=0, has_side_effects=True),
+        name="head",
+    )(nrm, dyo, pack, bias, seg)
+
+
+def sums_kernel(nz, nb, n_small, n_bias, mine, out, other, acc, slots, send, recv):
+    z, x, y, c = here(nz, nb)
+    ident = lambda z, x, y, c: (2 * z + x, 2 * y + c)
+    rounds = []
+    step = 1
+    while step < nz:
+        far = (z // step) % 2
+        rounds.append(((z + step - 2 * step * far, x, y, c), "z"))
+        step *= 2
+    rounds += [((z, 1 - x, y, c), "x"), ((z, x, 1 - y, c), "y"), ((z, x, y, 1 - c), "c")]
+    barrier = pltpu.get_barrier_semaphore()
+    for to, _ in rounds:
+        pl.semaphore_signal(barrier, inc=1, device_id=ident(*to), device_id_type=MESH)
+    pl.semaphore_wait(barrier, len(rounds))
+    acc[...] = mine[...]
+    biases = slice(n_small, n_small + n_bias)
+    done_z = False
+    copies = []
+    for r, (to, kind) in enumerate(rounds):
+        if kind != "z" and not done_z:
+            done_z = True
+            total = acc[biases, :]
+            acc[n_small + n_bias:, :] += jnp.sum(total * total) * (
+                (lax.broadcasted_iota(jnp.int32, (8, 128), 0) == 0)
+                & (lax.broadcasted_iota(jnp.int32, (8, 128), 1) == 0)
+            ).astype(F32)
+            out[biases, :] = total
+        slots[0, r] = acc[...]
+        copy = pltpu.make_async_remote_copy(
+            src_ref=slots.at[0, r], dst_ref=slots.at[1, r], send_sem=send.at[r], recv_sem=recv.at[r],
+            device_id=ident(*to), device_id_type=MESH)
+        copy.start()
+        copies.append(copy)
+        copy.wait_recv()
+        acc[...] += slots[1, r]
+        if kind == "x":
+            other[...] = slots[1, r, biases, :]
+    out[:n_small, :] = acc[:n_small, :]
+    out[n_small + n_bias:, :] = acc[n_small + n_bias:, :]
+    for copy in copies:
+        copy.wait_send()
+
+
+def sums(nz, nb, small, bias, squares):
+    pad = -bias.size % 1024
+    rows = [small.reshape(-1, 128), jnp.pad(bias, (0, pad)).reshape(-1, 128), jnp.pad(squares.reshape(1, 1), ((0, 7), (0, 127)))]
+    n_small, n_bias = rows[0].shape[0], rows[1].shape[0]
+    n = n_small + n_bias + 8
+    n_rounds = int(math.log2(nz)) + 3
+    vmem = pl.BlockSpec(memory_space=pltpu.VMEM)
+    dma = pltpu.SemaphoreType.DMA
+    out, other = pl.pallas_call(
+        functools.partial(sums_kernel, nz, nb, n_small, n_bias),
+        in_specs=[vmem],
+        out_specs=[vmem, vmem],
+        out_shape=[jax.ShapeDtypeStruct((n, 128), F32), jax.ShapeDtypeStruct((n_bias, 128), F32)],
+        scratch_shapes=[
+            pltpu.VMEM((n, 128), F32), pltpu.VMEM((2, n_rounds, n, 128), F32), dma((n_rounds,)), dma((n_rounds,))],
+        compiler_params=pltpu.CompilerParams(collective_id=1, has_side_effects=True),
+        name="sums",
+    )(jnp.concatenate(rows))
+    flat = lambda v: v.reshape(-1)[: bias.size]
+    return (out[:n_small].reshape(small.shape), flat(out[n_small:n_small + n_bias]), flat(other),
+            out[n_small + n_bias, 0])
+
+
 class Place:
     def __init__(self, nd, nb):
         self.nz, self.nb = nd // 2, nb
@@ -176,28 +434,6 @@
 
     def along_z(self, v, hops):
         return self.send(v, lambda z, x, y, c: (hops[z], x, y, c) if z in hops else None)
-
-
-def gather_tokens(at, own):
-    rows, block, d = own.shape
-    first = at.swap_first(own)
-    second = at.swap_second(own)
-    third = at.swap_second(first)
-    pieces = [own, first, second, third]
-    full = jnp.zeros((2, rows, at.nb, block, d), own.dtype)
-    c0 = at.c == 0
-    flips = [(0, 0), (jnp.where(c0, 1, 0), jnp.where(c0, 0, 1)), (jnp.where(c0, 0, 1), jnp.where(c0, 1, 0)), (1, 1)]
-    for piece, (fx, fy) in zip(pieces, flips):
-        for other in (0, 1):
-            here = at.swap_c(piece) if other else piece
-            if other:
-                gx, gy = (fy, fx)
-            else:
-                gx, gy = (fx, fy)
-            spot = (at.x + gx) % 2, 2 * ((at.y + gy) % 2) + (at.c + other) % 2
-            full = lax.dynamic_update_slice(
-                full, here[None, :, None], (spot[0], 0, spot[1], 0, 0))
-    return full
 
 
 def scatter_tokens(at, part):
@@ -216,44 +452,16 @@
     return pick(q, i, 0) + got.astype(F32)
 
 
+def over_z(at):
+    return [[2 * z + x for z in range(at.nz)] for x in range(2)]
+
+
 def gather_z(at, chunk):
-    if at.nz == 4:
-        odd = at.z % 2 == 1
-        got = at.along_z(chunk, {0: 1, 1: 0, 2: 3, 3: 2})
-        two = jnp.where(odd, jnp.concatenate([got, chunk]), jnp.concatenate([chunk, got]))
-        near = at.along_z(two, {1: 2, 2: 1})
-        far = at.along_z(near, {1: 0, 2: 3})
-        rest = jnp.where((at.z == 1) | (at.z == 2), near, far)
-        return jnp.where(at.z < 2, jnp.concatenate([two, rest]), jnp.concatenate([rest, two]))
-    n, cols = chunk.shape
-    full = jnp.zeros((at.nz * n, cols), chunk.dtype)
-    ring = {z: (z + 1) % at.nz for z in range(at.nz)}
-    for step in range(at.nz):
-        full = lax.dynamic_update_slice(full, chunk, (((at.z - step) % at.nz) * n, 0))
-        if step < at.nz - 1:
-            chunk = at.along_z(chunk, ring)
-    return full
+    return lax.all_gather(chunk, "dp", axis=0, tiled=True, axis_index_groups=over_z(at))
 
 
 def scatter_z(at, part):
-    n = part.shape[0] // at.nz
-    part = part.reshape(at.nz, n, part.shape[1])
-    pick = lambda v, i: lax.dynamic_index_in_dim(v, i, 0, keepdims=False)
-    if at.nz == 4:
-        half = at.z // 2
-        mine = lax.dynamic_slice_in_dim(part, 2 * half, 2, 0)
-        away = lax.dynamic_slice_in_dim(part, 2 - 2 * half, 2, 0)
-        got = at.along_z(away, {0: 1, 3: 2})
-        got = at.along_z((away.astype(F32) + got.astype(F32)).astype(LOW), {1: 2, 2: 1})
-        total = mine.astype(F32) + got.astype(F32)
-        got = at.along_z(pick(total, 1 - at.z % 2).astype(LOW), {0: 1, 1: 0, 2: 3, 3: 2})
-        return pick(total, at.z % 2) + got.astype(F32)
-    ring = {z: (z + 1) % at.nz for z in range(at.nz)}
-    total = pick(part, (at.z - 1) % at.nz).astype(F32)
-    for step in range(1, at.nz):
-        got = at.along_z(total.astype(LOW), ring)
-        total = pick(part, (at.z - 1 - step) % at.nz).astype(F32) + got.astype(F32)
-    return total
+    return lax.psum_scatter(part, "dp", scatter_dimension=0, tiled=True, axis_index_groups=over_z(at)).astype(F32)
 
 
 def adamw(weight, grad, first, second, rate, decay, count):
@@ -318,24 +526,27 @@
         shrink = lax.dynamic_slice_in_dim(shrink_weight.astype(LOW), h * hidden2, hidden2, 0).T
         return attend, expand, shrink
 
+    own, away = halves(at.x), halves(1 - at.x)
+    pack = jnp.where(x0, jnp.stack([own[0], away[0]]), jnp.stack([away[0], own[0]]))
+    biases = jnp.concatenate([attend_bias.reshape(-1), expand_bias]).astype(LOW)
+    n_bias = biases.size
+    biases = jnp.pad(biases, (0, -n_bias % 128)).reshape(1, -1)
+    tok, dy, attend, biases, segs = head(at.nz, nb, normed, out_grad, pack, biases, segments)
+    tok, dy = tok.reshape(tokens, d), dy.reshape(tokens, d)
+    segs = segs.reshape(2 * rows, length)
+    attend = attend.reshape(d, 4 * heads2)
     whole = []
-    for mine, theirs in zip(halves(at.x), halves(1 - at.x)):
+    for mine, theirs in zip(own[1:], away[1:]):
         got = at.swap_x(theirs)
         chunk = jnp.where(x0, jnp.concatenate([mine, got]), jnp.concatenate([got, mine]))
         whole.append(gather_z(at, chunk))
-    attend, expand, shrink = whole
-    biases = jnp.concatenate([attend_bias.reshape(-1), expand_bias]).astype(LOW)
-    biases = lax.all_gather(biases, "dp", axis=0)
+    expand, shrink = whole
+    biases = biases[:, 0, :n_bias]
     n_att = attend_bias.shape[1]
     bias_att = jnp.moveaxis(biases[:, : 3 * n_att].reshape(nd, 3, n_att), 0, 1).reshape(3, -1)
     bias_att = lax.dynamic_slice_in_dim(bias_att, at.x * heads2, heads2, 1).astype(F32)
     bias_exp = lax.dynamic_slice_in_dim(
         biases[:, 3 * n_att:].reshape(-1), at.x * hidden2, hidden2, 0).astype(F32)
-
-    tok = gather_tokens(at, normed).reshape(tokens, d)
-    dy = gather_tokens(at, out_grad).reshape(tokens, d)
-    got = at.swap_x(segments)
-    segs = jnp.where(x0, jnp.concatenate([segments, got]), jnp.concatenate([got, segments]))
 
     att_w, wo_t = attend[:, : 3 * heads2], attend[:, 3 * heads2:]
     proj = dot(tok, att_w, ((1,), (0,))) + bias_att.reshape(-1)
@@ -390,20 +601,17 @@
     back = out_grad.astype(F32)
     d_rows = (d_rows + back).astype(LOW)
 
-    sum_att = jnp.sum(d_proj.astype(F32), 0).reshape(3, heads2)
-    sum_exp = jnp.sum(d_up.astype(F32), 0)
-    spread_att = lax.dynamic_update_slice(jnp.zeros((3, 2 * heads2), F32), sum_att, (0, at.x * heads2))
-    spread_exp = lax.dynamic_update_slice(jnp.zeros((2 * hidden2,), F32), sum_exp, (at.x * hidden2,))
-    spread = lax.psum(jnp.concatenate([spread_att.reshape(-1), spread_exp]), "dp")
+    small = jnp.stack([grad_gain, grad_shift, jnp.sum(back, (0, 1))])
+    pieces = (lo_a, hi_a, lo_s, hi_s, lo_e, hi_e)
+    squares = sum(jnp.sum(piece * piece) for piece in pieces)
+    bias = jnp.concatenate([jnp.sum(d_proj.astype(F32), 0), jnp.sum(d_up.astype(F32), 0)])
+    g_small, bias, bias_other, squares = sums(at.nz, nb, small, bias, squares)
+    both = jnp.where(x0, jnp.stack([bias, bias_other]), jnp.stack([bias_other, bias]))
     n_exp = expand_bias.shape[0]
-    g_bias_att = lax.dynamic_slice_in_dim(
-        spread[: 6 * heads2].reshape(3, 2 * heads2), at.dp * n_att, n_att, 1)
-    g_bias_exp = lax.dynamic_slice_in_dim(spread[6 * heads2:], at.dp * n_exp, n_exp, 0)
-
-    small = jnp.stack([grad_gain, grad_shift, jnp.sum(back, (0, 1))])
-    pieces = (lo_a, hi_a, lo_s, hi_s, lo_e, hi_e, g_bias_att, g_bias_exp)
-    squares = sum(jnp.sum(piece * piece) for piece in pieces)
-    g_small, squares = lax.psum((small, squares), AXES)
+    full_att = jnp.moveaxis(both[:, : 3 * heads2].reshape(2, 3, heads2), 0, 1).reshape(3, 2 * heads2)
+    g_bias_att = lax.dynamic_slice_in_dim(full_att, at.dp * n_att, n_att, 1)
+    g_bias_exp = lax.dynamic_slice_in_dim(both[:, 3 * heads2:].reshape(-1), at.dp * n_exp, n_exp, 0)
+
     norm_value = jnp.sqrt(squares + jnp.sum(g_small * g_small))
     size = 4 * d * d + 2 * d * 2 * hidden2 * nb
     factor = jnp.minimum(1.0, math.sqrt(size) / norm_value)

time: 974 us -> 626 us (0.64)
  blocking collectives: 195 us -> 0 us
  Pallas kernels: 30.8 us -> 190 us
  starting transfers between devices: 163 us -> 15.3 us
  waiting for transfers between devices: 193 us -> 70.6 us
  other arithmetic: 120 us -> 87.5 us
  local copies, waits for them, and re-layouts: 99.8 us -> 87.2 us
  between operations: 9.77 us -> 21.4 us
    psum x2 -> x0, blocking collectives: 163 us -> none  [the longest x1 115 us: on_device(): lax.psum(jnp.concatenate([spread_att.reshape(-1), spread_exp]), 'dp')]
    pallas_call x0 -> x2, Pallas kernels: none -> 160 us  [the longest x1 141 us: head(): pl.pallas_call(functools.partial(head_kernel, nz, nb), in_specs=[anywhere...]
    ppermute x45 -> x11, starting transfers between devices: 163 us -> 14.4 us  [send(): return lax.ppermute(value, AXES, perm=pairs)]
    ppermute x45 -> x11, waiting for transfers between devices: 193 us -> 62.1 us  [send(): return lax.ppermute(value, AXES, perm=pairs)]
    all_gather x1 -> x0, blocking collectives: 32 us -> none  [on_device(): biases = lax.all_gather(biases, 'dp', axis=0)]
    dynamic_slice x3 -> x12, local copies, waits for them, and re-layouts: 6.06 us -> 20.9 us  [the longest x4 14.9 us: scatter_tokens(): lax.dynamic_index_in_dim(v, i, axis, keepdims=False)]
    dynamic_update_slice x17 -> x0, local copies, waits for them, and re-layouts: 14.1 us -> none  [the longest x15 13.7 us: gather_tokens(): lax.dynamic_update_slice(full, here[None, :, None], (spot[0], 0, spot[1],...]
    add x6 -> x0, other arithmetic: 13.2 us -> none  [the longest x3 8.26 us: scatter_z(): total = mine.astype(F32) + got.astype(F32)]
  transfers between devices with their start and end apart: 45 -> 16, of which waited for: 12 -> 6; matrix products, arithmetic and copies ran while one was open for 28% -> 41% of each run, Pallas kernels for 3% -> 28%
where the time goes in v2:
time: 626 us; the launch traced here: 619 us
  Pallas kernels  190 us (30%)
  matrix products  147 us (23%)
  other arithmetic  87.5 us (14%)
  local copies, waits for them, and re-layouts  87.2 us (14%)
  waiting for transfers between devices  70.6 us (11%)
  between operations  21.4 us (3%)
  starting transfers between devices  15.3 us (2%)
    dot_general x12, matrix products, dot(): lax.dot_general(a, b, (dims, ((), ())), preferred_element_type=F32)  147 us
    pallas_call x1, Pallas kernels, head(): pl.pallas_call(functools.partial(head_kernel, nz, nb), in_specs=[anywhere...  141 us
    ppermute x11, waiting for transfers between devices, send(): return lax.ppermute(value, AXES, perm=pairs)  62.1 us
    unnamed x141, local copies, waits for them, and re-layouts  49.6 us
    pallas_call x1, Pallas kernels, attention(): pl.pallas_call(attention_kernel, grid=(rows, pairs), in_specs=[part(0), p...  30.4 us
    pallas_call x1, Pallas kernels, sums(): pl.pallas_call(functools.partial(sums_kernel, nz, nb, n_small, n_bias), i...  18.5 us
    dynamic_slice x4, local copies, waits for them, and re-layouts, scatter_tokens(): lax.dynamic_index_in_dim(v, i, axis, keepdims=False)  14.9 us
    ppermute x11, starting transfers between devices, send(): return lax.ppermute(value, AXES, perm=pairs)  14.4 us
  transfers between devices with their start and end apart: 16, of which 6 were waited for; matrix products, arithmetic and copies ran while one was open for 41% of the time, Pallas kernels for 28%

profile of v2, /device:TPU:0, one launch (start us, length us, event | category | flops | bytes accessed | tf_op | source)
XLA Modules:
  0.0 618.9 jit_solution(12915201375552709804)
XLA Ops:
  10.6 2.9 collective-permute-start
  13.5 12.1 %collective-permute-done = bf16[256,1024]{0,1:T(8,128)(2,1)S(1)} collective-permute-done((bf16[256,1024]{0,1:T(8,128)(2,1)}, bf16[256,1024]{0,1:T(8,128)(2,1)S(1)}, u32[]{:S(2)}, u32[]{:S(2)}) %collective-permute-start) | collective-permute-done | bytes 524320 | tf_op jit(solution)/shard_map/ppermute | solution.py:421
  38.5 141.2 %head.1 = (bf16[2,2,4,128,2048]{4,3,2,1,0:T(8,128)(2,1)}, bf16[2,2,4,128,2048]{4,3,2,1,0:T(8,128)(2,1)}, bf16[4,2,256,1024]{3,2,1,0:T(8,128)(2,1)}, bf16[8,1,512]{2,1,0:T(2,128)(2,1)}, s32[2,2,512]{2,1,0:T(2,128)}) custom-call(bf16[2,128,2048]{2,1,0:T(8,128)(2,1)} %fusion.21.nrm, bf16[2,128,2048]{2,1,0:T(8,128)(2,1)} %dyo.1, ...), custom_call_target="tpu_custom_call" | custom-call | tf_op jit(solution)/shard_map/head/pallas_call | solution.py:320
  182.4 2.6 reshape_reshape.16.segc_ref
  187.8 6.9 %convolution_convert_fusion.4.d_ref = bf16[2048,256]{1,0:T(8,128)(2,1)} fusion(bf16[2048,2048]{1,0:T(8,128)(2,1)} %bitcast.239, bf16[2048,1024]{1,0:T(8,128)(2,1)} %bitcast.208), kind=kOutput, calls=%fused_computation.46 | convolution fusion | flops 2148007936 | bytes 10485760 | tf_op jit(solution)/shard_map/dot_general | solution.py:62
  194.7 5.8 fusion.34
  200.5 2.5 maximum_select_fusion.2
  203.6 11.8 %broadcast_add_fusion.q_ref.k_ref.v_ref = f32[2048,768]{1,0:T(8,128)} fusion(f32[768]{0:T(1024)S(1)} %reshape.262, bf16[2048,2048]{1,0:T(8,128)(2,1)} %bitcast.233, bf16[2048,1024]{1,0:T(8,128)(2,1)} %bitcast.209), kind=kOutput, calls=%fused_computation.32 | convolution fusion | flops 6444023808 | bytes 17828864 | tf_op jit(solution)/shard_map/dot_general | solution.py:62
  215.3 30.4 %shard_map.447 = (bf16[2048,256]{1,0:T(8,128)(2,1)}, bf16[2048,256]{1,0:T(8,128)(2,1)}, bf16[2048,256]{1,0:T(8,128)(2,1)}, bf16[2048,256]{1,0:T(8,128)(2,1)}) custom-call(f32[2048,768]{1,0:T(8,128)} %broadcast_add_fusion.q_ref.k_ref.v_ref, f32[2048,768]{1,0:T(8,128)} %broadcast_add_fusion.q_ref.k_ref.v_ref, f32[2048,768]{1,0:T(8,128)} %broadcast_add_fusion.q_ref.k_ref.v_ref, ...), custom_call_target="tpu_custom_call" | custom-call | flops 3758096384 | bytes 12582912 | tf_op jit(solution)/shard_map/pallas_call | solution.py:128
  248.6 7.0 %convolution_convert_fusion.3 = bf16[2048,256]{0,1:T(8,128)(2,1)S(1)} fusion(bf16[2048,2048]{1,0:T(8,128)(2,1)} %bitcast.240, bf16[2048,256]{1,0:T(8,128)(2,1)S(1)} %copy-done.27), kind=kOutput, calls=%fused_computation.45 | convolution fusion | flops 2148007936 | bytes 10485760 | tf_op jit(solution)/shard_map/dot_general | solution.py:62
  255.7 7.1 %convolution_convert_fusion.2 = bf16[2048,768]{0,1:T(8,128)(2,1)S(1)} fusion(bf16[2048,2048]{1,0:T(8,128)(2,1)S(1)} %bitcast.238, bf16[2048,768]{1,0:T(8,128)(2,1)S(1)} %constant_dynamic-update-slice_fusion), kind=kOutput, calls=%fused_computation.31 | convolution fusion | flops 6444023808 | bytes 14680064 | tf_op jit(solution)/shard_map/dot_general | solution.py:62
  265.5 9.8 %fusion.40 = f32[2048,2048]{1,0:T(8,128)} fusion(bf16[2048,256]{1,0:T(8,128)(2,1)} %get-tuple-element.44, bf16[2048,1024]{1,0:T(8,128)(2,1)} %bitcast.210), kind=kOutput, calls=%fused_computation.104 | convolution fusion | flops 2147483648 | bytes 18874368 | tf_op jit(solution)/shard_map/dot_general | solution.py:62
  275.3 9.6 %fusion.11 = f32[2048,2048]{1,0:T(8,128)} fusion(bf16[2048,768]{1,0:T(8,128)(2,1)S(1)} %constant_dynamic-update-slice_fusion, bf16[2048,1024]{1,0:T(8,128)(2,1)S(1)} %bitcast.211), kind=kOutput, calls=%fused_computation.40 | convolution fusion | flops 6442450944 | bytes 23068672 | tf_op jit(solution)/shard_map/dot_general | solution.py:62
  284.9 12.5 %fusion.74 = f32[2048,1024]{1,0:T(8,128)S(1)} fusion(bf16[2048,2048]{1,0:T(8,128)(2,1)} %bitcast.234, bf16[2048,1024]{0,1:T(8,128)(2,1)} %all-gather.3.cloned.1.call-done), kind=kOutput, calls=%fused_computation.216 | convolution fusion | flops 8589934592 | bytes 20971520 | tf_op jit(solution)/shard_map/dot_general | solution.py:62
  297.5 3.2 copy-done.53
  300.7 13.3 %convolution_convert_fusion.1 = bf16[2048,1024]{1,0:T(8,128)(2,1)} fusion(bf16[2048,2048]{1,0:T(8,128)(2,1)} %bitcast.241, f32[2048,1024]{1,0:T(8,128)S(1)} %fusion.74, f32[1024]{0:T(1024)S(1)} %dynamic-slice_convert_fusion.2), kind=kOutput, calls=%fused_computation.30 | convolution fusion | flops 8613003264 | bytes 20975616 | tf_op jit(solution)/shard_map/dot_general | solution.py:62
  314.1 21.5 %convert_reduce_fusion = (f32[1024]{0:T(1024)S(1)}, bf16[2048,1024]{1,0:T(8,128)(2,1)}) fusion(f32[2048,1024]{1,0:T(8,128)} %copy-done.53, f32[1024]{0:T(1024)S(1)} %dynamic-slice_convert_fusion.2, bf16[2048,2048]{1,0:T(8,128)(2,1)} %bitcast.242, bf16[2048,1024]{0,1:T(8,128)(2,1)} %all-gather.5.cloned.1.call-done), kind=kOutput, calls=%fused_computation.13 | convolution fusion | flops 8636070912 | bytes 25174016 | tf_op jit(solution)/shard_map/dot_general | solution.py:62
  335.6 14.5 %add_convert_fusion = bf16[2048,2048]{1,0:T(8,128)(2,1)S(1)} fusion(f32[2048,2048]{1,0:T(8,128)} %fusion.11, bf16[2048,1024]{1,0:T(8,128)(2,1)} %get-tuple-element.189, bf16[2048,1024]{0,1:T(8,128)(2,1)} %all-gather.3.cloned.1.call-done), kind=kOutput, calls=%fused_computation | convolution fusion | flops 8598323200 | bytes 33554432 | tf_op jit(solution)/shard_map/dot_general | solution.py:62
  350.1 3.2 constant_dynamic-slice_fusion.8
  357.1 19.9 %add_convert_fusion.1 = bf16[2048,2048]{1,0:T(8,128)(2,1)} fusion(f32[2048,2048]{1,0:T(8,128)} %fusion.40, bf16[2048,1024]{0,1:T(8,128)(2,1)S(1)} %copy-done.51, f32[2048,1024]{1,0:T(8,128)} %copy-done.53, f32[1024]{0:T(1024)S(1)} %dynamic-slice_convert_fusion.2), kind=kOutput, calls=%fused_computation.1 | convolution fusion | flops 8619294720 | bytes 37752832 | tf_op jit(solution)/shard_map/dot_general | solution.py:62
  377.0 6.8 %constant_dynamic-slice_fusion.10 = (bf16[2,2,2,1,128,2048]{5,4,3,2,1,0:T(8,128)(2,1)}, bf16[2,2,2,1,128,2048]{5,4,3,2,1,0:T(8,128)(2,1)S(1)}) fusion(bf16[2,2,2,2,128,2048]{5,4,3,2,1,0:T(8,128)(2,1)} %bitcast.203, s32[]{:T(128)S(6)} %select_n.223, s32[]{:T(128)S(6)} %select_n.224), kind=kLoop, calls=%fused_computation.151 | loop fusion | bytes 16777224 | tf_op jit(solution)/shard_map/jit(dynamic_index_in_dim)/dynamic_slice | solution.py:442
  387.5 12.7 %convolution_convert_fusion = bf16[2048,1024]{1,0:T(8,128)(2,1)} fusion(bf16[2048,2048]{1,0:T(8,128)(2,1)} %bitcast.235, bf16[2048,1024]{1,0:T(8,128)(2,1)S(1)} %copy-done.52), kind=kOutput, calls=%fused_computation.29 | convolution fusion | flops 8592031744 | bytes 16777216 | tf_op jit(solution)/shard_map/dot_general | solution.py:62
  403.3 3.2 copy.93
  406.5 3.0 copy.94
  411.4 2.9 copy.98
  414.2 2.8 reshape.266
  418.6 5.4 convert_add_fusion
  427.2 4.0 convert_add_fusion.1
  437.5 14.5 %collective-permute-done.6 = bf16[2,2,128,2048]{3,2,1,0:T(8,128)(2,1)} collective-permute-done((bf16[2,2,128,2048]{3,2,1,0:T(8,128)(2,1)}, bf16[2,2,128,2048]{3,2,1,0:T(8,128)(2,1)}, u32[]{:S(2)}, u32[]{:S(2)}) %collective-permute-start.6) | collective-permute-done | bytes 2097184 | tf_op jit(solution)/shard_map/ppermute | solution.py:421
  452.0 2.8 fusion.8
  457.8 27.8 %collective-permute-done.3 = bf16[2,2,128,2048]{3,2,1,0:T(8,128)(2,1)S(1)} collective-permute-done((bf16[2,2,128,2048]{3,2,1,0:T(8,128)(2,1)S(1)}, bf16[2,2,128,2048]{3,2,1,0:T(8,128)(2,1)S(1)}, u32[]{:S(2)}, u32[]{:S(2)}) %collective-permute-start.3) | collective-permute-done | bytes 2097184 | tf_op jit(solution)/shard_map/ppermute | solution.py:421
  496.5 3.2 fusion.25
  499.8 4.1 collective-permute-done.4
  503.8 3.1 convert_reduce_fusion.3
  511.2 8.4 %reduce-scatter.8.cloned.1.call-done = bf16[512,1024]{1,0:T(8,128)(2,1)} async-done(((bf16[2048,1024]{1,0:T(8,128)(2,1)}), bf16[512,1024]{1,0:T(8,128)(2,1)}) %reduce-scatter.8.cloned.1.call-update) | async-done | bytes 1048592 | tf_op jit(solution)/shard_map/reduce_scatter | solution.py:464
  529.0 3.6 multiply_reduce_fusion.3
  534.0 3.6 collective-permute-done.10
  537.6 3.5 multiply_reduce_fusion.1
  543.0 18.5 %sums.1 = (f32[72,128]{1,0:T(8,128)}, f32[16,128]{1,0:T(8,128)}) custom-call(f32[72,128]{1,0:T(8,128)} %select_maximum_fusion.mine), custom_call_target="tpu_custom_call" | custom-call | tf_op jit(solution)/shard_map/sums/pallas_call | solution.py:390
  567.6 5.0 multiply_subtract_fusion.2
  572.6 3.2 copy.103
  575.8 6.4 %multiply_subtract_fusion.1 = (f32[256,2048]{0,1:T(8,128)}, f32[256,2048]{0,1:T(8,128)}, f32[256,2048]{0,1:T(8,128)}) fusion(f32[256,2048]{0,1:T(8,128)S(1)} %copy-done.3, f32[256,1024]{0,1:T(8,128)S(1)} %copy-done.22, f32[256,1024]{0,1:T(8,128)} %get-tuple-element.151, f32[]{:T(128)S(6)} %min.3, f32[256,2048]{0,1:T(8,128)} %copy.97, f32[256,2048]{0,1:T(8,128)} %copy.98), kind=kLoop, calls=%fused_computation.73 | loop fusion | flops 8388608 | bytes 14680068 | tf_op jit(solution)/shard_map/sub | solution.py:473
  584.2 3.1 convert_element_type.227
  588.5 3.0 copy.105
  591.5 3.2 copy.107
  594.6 2.9 copy.106
  601.8 2.7 fusion.63
  604.5 6.5 %fusion.61 = (bf16[2048,256]{1,0:T(8,128)(2,1)}, f32[2048,256]{1,0:T(8,128)}, f32[2048,256]{1,0:T(8,128)}, f32[2048,256]{1,0:T(8,128)}) fusion(f32[2048,256]{1,0:T(8,128)S(1)} %copy-done.8, f32[256,1024]{0,1:T(8,128)S(1)} %copy-done.20, f32[256,1024]{0,1:T(8,128)S(1)} %copy-done.21, f32[]{:T(128)S(6)} %min.3, f32[2048,256]{1,0:T(8,128)} %param.40, ...), kind=kLoop, calls=%fused_computation.210 | loop fusion | flops 8912896 | bytes 15728644 | tf_op jit(solution)/shard_map/convert_element_type | solution.py:644
  (255 shorter events, 89.5 us)
Async XLA Ops:
  7.2 277.7 %all-gather.3.cloned.1.call-start = ((), (), s32[]{:S(2)}) async-start(), calls=%async_computation.3 | async-start | bytes 5242880 | tf_op jit(solution)/shard_map/all_gather | solution.py:460
  9.2 18.9 %copy-start.2 = (f32[256,2048]{0,1:T(8,128)}, f32[256,2048]{0,1:T(8,128)S(1)}, u32[]{:S(2)}) copy-start(f32[256,2048]{0,1:T(8,128)S(1)} %copy.81) | copy-start | bytes 6291460
  10.6 15.1 %collective-permute-start = (bf16[256,1024]{0,1:T(8,128)(2,1)}, bf16[256,1024]{0,1:T(8,128)(2,1)S(1)}, u32[]{:S(2)}, u32[]{:S(2)}) collective-permute-start(bf16[256,1024]{0,1:T(8,128)(2,1)} %get-tuple-element.168), channel_id=1, source_target_pairs={{0,4},{1,5},{2,6},{3,7},{4,0},{5,1},{6,2},{7,3},{8,12},{9,13},{10,... | collective-permute-start | bytes 1572872 | tf_op jit(solution)/shard_map/ppermute | solution.py:421
  28.1 4.6 copy-start.47
  28.1 4.6 copy-start.43
  28.1 5.3 copy-start.24
  28.1 5.4 copy-start.14
  28.1 286.0 %all-gather.5.cloned.1.call-start = ((), (), s32[]{:S(2)}) async-start(), calls=%async_computation.4 | async-start | bytes 5242880 | tf_op jit(solution)/shard_map/all_gather | solution.py:460
  30.9 169.6 %collective-permute-start.1 = (bf16[256,1024]{0,1:T(8,128)(2,1)}, bf16[256,1024]{0,1:T(8,128)(2,1)}, u32[]{:S(2)}, u32[]{:S(2)}) collective-permute-start(bf16[256,1024]{0,1:T(8,128)(2,1)} %get-tuple-element.170), channel_id=1, source_target_pairs={{0,4},{1,5},{2,6},{3,7},{4,0},{5,1},{6,2},{7,3},{8,12},{9,13},{10,... | collective-permute-start | bytes 1572872 | tf_op jit(solution)/shard_map/ppermute | solution.py:421
  203.0 211.2 %reduce-scatter.4.cloned.1.call-start = ((), (), s32[]{:S(2)}) async-start(), calls=%async_computation.5 | async-start | bytes 5242880 | tf_op jit(solution)/shard_map/reduce_scatter | solution.py:464
  248.5 7.1 %slice-start.1 = ((s8[8388608]{0:T(1024)(128)(4,1)}), s8[4194304]{0:T(1024)(128)(4,1)S(1)}, s32[]{:S(2)}) async-start(s8[8388608]{0:T(1024)(128)(4,1)} %bitcast.236), calls=%async_computation.9 | async-start | bytes 8388608
  248.6 26.7 %copy-start.18 = (bf16[2048,768]{1,0:T(8,128)(2,1)}, bf16[2048,768]{1,0:T(8,128)(2,1)S(1)}, u32[]{:S(2)}) copy-start(bf16[2048,768]{1,0:T(8,128)(2,1)S(1)} %constant_dynamic-update-slice_fusion) | copy-start | bytes 9437188
  248.6 7.0 %slice-start.2 = ((s8[8388608]{0:T(1024)(128)(4,1)}), s8[4194304]{0:T(1024)(128)(4,1)S(1)}, s32[]{:S(2)}) async-start(s8[8388608]{0:T(1024)(128)(4,1)} %bitcast.236), calls=%async_computation.10 | async-start | bytes 8388608
  265.1 241.9 %reduce-scatter.6.cloned.1.call-start = ((), (), s32[]{:S(2)}) async-start(), calls=%async_computation.6 | async-start | bytes 5242880 | tf_op jit(solution)/shard_map/reduce_scatter | solution.py:464
  265.5 9.8 %copy-start.30 = (bf16[4,2,256,1024]{3,2,1,0:T(8,128)(2,1)S(1)}, bf16[4,2,256,1024]{3,2,1,0:T(8,128)(2,1)}, u32[]{:S(2)}) copy-start(bf16[4,2,256,1024]{3,2,1,0:T(8,128)(2,1)} %get-tuple-element.41) | copy-start | bytes 12582916
  314.0 205.6 %reduce-scatter.8.cloned.1.call-start = ((), (), s32[]{:S(2)}) async-start(), calls=%async_computation.7 | async-start | bytes 5242880 | tf_op jit(solution)/shard_map/reduce_scatter | solution.py:464
  353.4 3.7 copy-start.51
  355.8 62.7 %collective-permute-start.5 = (bf16[2,2,2,128,2048]{4,3,1,2,0:T(8,128)(2,1)}, bf16[2,2,2,128,2048]{4,3,1,2,0:T(8,128)(2,1)}, u32[]{:S(2)}, u32[]{:S(2)}) collective-permute-start(bf16[2,2,2,128,2048]{4,3,1,2,0:T(8,128)(2,1)} %bitcast.193), channel_id=1, source_target_pairs={{0,1},{1,0},{2,3},{3,2},{4,5},{5,4},{6,7},{7,6},{8,9},{9,8},{10,11... | collective-permute-start | bytes 12582920 | tf_op jit(solution)/shard_map/ppermute | solution.py:421
  383.8 3.7 copy-start.52
  386.2 40.9 %collective-permute-start.2 = (bf16[2,2,2,128,2048]{4,3,1,2,0:T(8,128)(2,1)}, bf16[2,2,2,128,2048]{4,3,1,2,0:T(8,128)(2,1)}, u32[]{:S(2)}, u32[]{:S(2)}) collective-permute-start(bf16[2,2,2,128,2048]{4,3,1,2,0:T(8,128)(2,1)} %bitcast.194), channel_id=1, source_target_pairs={{0,1},{1,0},{2,3},{3,2},{4,5},{5,4},{6,7},{7,6},{8,9},{9,8},{10,11... | collective-permute-start | bytes 12582920 | tf_op jit(solution)/shard_map/ppermute | solution.py:421
  403.3 6.2 %copy-start.26 = (f32[256,2048]{1,0:T(8,128)S(1)}, f32[256,2048]{1,0:T(8,128)}, u32[]{:S(2)}) copy-start(f32[256,2048]{1,0:T(8,128)} %param.38) | copy-start | bytes 6291460
  418.1 16.7 %collective-permute-start.8 = (bf16[256,1024]{0,1:T(8,128)(2,1)S(1)}, bf16[256,1024]{0,1:T(8,128)(2,1)S(1)}, u32[]{:S(2)}, u32[]{:S(2)}) collective-permute-start(bf16[256,1024]{0,1:T(8,128)(2,1)S(1)} %bitcast.207), channel_id=1, source_target_pairs={{0,4},{1,5},{2,6},{3,7},{4,0},{5,1},{6,2},{7,3},{8,12},{9,13},{10,... | collective-permute-start | bytes 1572872 | tf_op jit(solution)/shard_map/ppermute | solution.py:421
  425.6 26.4 %collective-permute-start.6 = (bf16[2,2,128,2048]{3,2,1,0:T(8,128)(2,1)}, bf16[2,2,128,2048]{3,2,1,0:T(8,128)(2,1)}, u32[]{:S(2)}, u32[]{:S(2)}) collective-permute-start(bf16[2,2,128,2048]{3,2,1,0:T(8,128)(2,1)} %fusion.7), channel_id=1, source_target_pairs={{0,2},{1,5},{2,0},{3,7},{4,6},{5,1},{6,4},{7,3},{8,10},{9,13},{10,... | collective-permute-start | bytes 6291464 | tf_op jit(solution)/shard_map/ppermute | solution.py:421
  431.6 54.0 %collective-permute-start.3 = (bf16[2,2,128,2048]{3,2,1,0:T(8,128)(2,1)S(1)}, bf16[2,2,128,2048]{3,2,1,0:T(8,128)(2,1)S(1)}, u32[]{:S(2)}, u32[]{:S(2)}) collective-permute-start(bf16[2,2,128,2048]{3,2,1,0:T(8,128)(2,1)S(1)} %fusion.9), channel_id=1, source_target_pairs={{0,2},{1,5},{2,0},{3,7},{4,6},{5,1},{6,4},{7,3},{8,10},{9,13},{10,... | collective-permute-start | bytes 6291464 | tf_op jit(solution)/shard_map/ppermute | solution.py:421
  456.2 40.3 %collective-permute-start.7 = (bf16[2,128,2048]{2,1,0:T(8,128)(2,1)}, bf16[2,128,2048]{2,1,0:T(8,128)(2,1)}, u32[]{:S(2)}, u32[]{:S(2)}) collective-permute-start(bf16[2,128,2048]{2,1,0:T(8,128)(2,1)} %fusion.39), channel_id=1, source_target_pairs={{0,4},{1,3},{2,6},{3,1},{4,0},{5,7},{6,2},{7,5},{8,12},{9,11},{10,... | collective-permute-start | bytes 3145736 | tf_op jit(solution)/shard_map/ppermute | solution.py:421
  488.8 7.7 %copy-start.1 = (bf16[2,128,2048]{2,1,0:T(8,128)(2,1)S(1)}, bf16[2,128,2048]{2,1,0:T(8,128)(2,1)}, u32[]{:S(2)}) copy-start(bf16[2,128,2048]{2,1,0:T(8,128)(2,1)} %param.24) | copy-start | bytes 3145732
  488.8 7.7 %copy-start.32 = (f32[1,2048]{1,0:T(1,128)S(1)}, f32[1,2048]{1,0:T(1,128)}, u32[]{:S(2)}) copy-start(f32[1,2048]{1,0:T(1,128)} %copy-done.31) | copy-start | bytes 24580
  488.8 7.7 %copy-start.40 = (f32[2,128]{1,0:T(2,128)S(1)}, f32[2,128]{1,0:T(2,128)}, u32[]{:S(2)}) copy-start(f32[2,128]{1,0:T(2,128)} %copy-done.39) | copy-start | bytes 3076
  488.8 7.7 %copy-start.42 = (f32[2,128]{1,0:T(2,128)S(1)}, f32[2,128]{1,0:T(2,128)}, u32[]{:S(2)}) copy-start(f32[2,128]{1,0:T(2,128)} %copy-done.41) | copy-start | bytes 3076
  489.0 14.9 %collective-permute-start.4 = (bf16[2,128,2048]{2,1,0:T(8,128)(2,1)S(1)}, bf16[2,128,2048]{2,1,0:T(8,128)(2,1)S(1)}, u32[]{:S(2)}, u32[]{:S(2)}) collective-permute-start(bf16[2,128,2048]{2,1,0:T(8,128)(2,1)S(1)} %fusion.38), channel_id=1, source_target_pairs={{0,4},{1,3},{2,6},{3,1},{4,0},{5,7},{6,2},{7,5},{8,12},{9,11},{10,... | collective-permute-start | bytes 3145736 | tf_op jit(solution)/shard_map/ppermute | solution.py:421
  496.5 7.3 %copy-start.6 = (f32[2,2,128,2048]{3,2,1,0:T(8,128)S(1)}, f32[2,2,128,2048]{3,2,1,0:T(8,128)}, u32[]{:S(2)}) copy-start(f32[2,2,128,2048]{3,2,1,0:T(8,128)} %copy-done.5) | copy-start | bytes 12582916
  496.5 7.3 %copy-start.23 = (bf16[2,128,2048]{2,1,0:T(8,128)(2,1)S(1)}, bf16[2,128,2048]{2,1,0:T(8,128)(2,1)}, u32[]{:S(2)}) copy-start(bf16[2,128,2048]{2,1,0:T(8,128)(2,1)} %dyo.1) | copy-start | bytes 3145732
  496.5 7.3 %copy-start.36 = (f32[1,2048]{1,0:T(1,128)S(1)}, f32[1,2048]{1,0:T(1,128)}, u32[]{:S(2)}) copy-start(f32[1,2048]{1,0:T(1,128)} %get-tuple-element.182) | copy-start | bytes 24580
  509.5 19.5 %collective-permute-start.9 = (bf16[256,1024]{0,1:T(8,128)(2,1)}, bf16[256,1024]{0,1:T(8,128)(2,1)}, u32[]{:S(2)}, u32[]{:S(2)}) collective-permute-start(bf16[256,1024]{0,1:T(8,128)(2,1)} %bitcast.163), channel_id=1, source_target_pairs={{0,4},{1,5},{2,6},{3,7},{4,0},{5,1},{6,2},{7,3},{8,12},{9,13},{10,... | collective-permute-start | bytes 1572872 | tf_op jit(solution)/shard_map/ppermute | solution.py:421
  523.5 14.0 %collective-permute-start.10 = (bf16[256,1024]{0,1:T(8,128)(2,1)}, bf16[256,1024]{0,1:T(8,128)(2,1)}, u32[]{:S(2)}, u32[]{:S(2)}) collective-permute-start(bf16[256,1024]{0,1:T(8,128)(2,1)} %bitcast.162), channel_id=1, source_target_pairs={{0,4},{1,5},{2,6},{3,7},{4,0},{5,1},{6,2},{7,3},{8,12},{9,13},{10,... | collective-permute-start | bytes 1572872 | tf_op jit(solution)/shard_map/ppermute | solution.py:421
  529.0 38.6 %copy-start.16 = (f32[3,256,512]{1,2,0:T(8,128)S(1)}, f32[3,256,512]{1,2,0:T(8,128)}, u32[]{:S(2)}) copy-start(f32[3,256,512]{1,2,0:T(8,128)} %copy.96) | copy-start | bytes 4718596
  529.0 38.6 %copy-start.17 = (f32[3,256,512]{1,2,0:T(8,128)S(1)}, f32[3,256,512]{1,2,0:T(8,128)}, u32[]{:S(2)}) copy-start(f32[3,256,512]{1,2,0:T(8,128)} %copy.93) | copy-start | bytes 4718596
  565.5 7.1 %copy-start.35 = (f32[2,1792]{1,0:T(2,128)}, f32[2,1792]{1,0:T(2,128)S(1)}, u32[]{:S(2)}) copy-start(f32[2,1792]{1,0:T(2,128)S(1)} %maximum_select_fusion.3) | copy-start | bytes 43012
  584.2 7.3 %copy-start.11 = (f32[256,2048]{1,0:T(8,128)}, f32[256,2048]{1,0:T(8,128)S(1)}, u32[]{:S(2)}) copy-start(f32[256,2048]{1,0:T(8,128)S(1)} %copy.104) | copy-start | bytes 6291460
  591.5 6.2 copy-start.12
  597.6 3.5 copy-start.44
  597.6 3.5 copy-start.45
  597.6 3.5 copy-start.46
  597.6 4.2 copy-start.25
  597.6 4.2 copy-start.29
  599.7 4.8 copy-start.8
  599.7 4.8 copy-start.20
  599.7 4.8 copy-start.21
  (25 other events, 54.5 us)
Sparse Core Ops, SparseCore 0:
  28.2 93.3 all-gather.2
  203.1 79.8 all-gather.4
  285.3 75.2 reduce-scatter.3
  362.9 77.2 reduce-scatter.5
  442.4 77.2 reduce-scatter.7
